TPU v7x, 1024 devices: a whole 8x8x8 slice. The times are simulated.
1024 devices in a mesh: gx: 16 (over y, z_lo), gy: 8 (over x), gz: 8 (over z_hi, core).
Axes of the slice: x: 8, y: 8, z: 8 (z_hi: 4, z_lo: 2; z = z_hi * 2 + z_lo), core: 2. Of those that a mesh axis runs over, the one named last changes fastest.
Arguments:
- positions: float32 [3, 16, 8, 8, 512], P(None, 'gx', 'gy', 'gz'), may hold values from 0 to 1
- velocities: float32 [3, 16, 8, 8, 512], P(None, 'gx', 'gy', 'gz'), may hold values from -1.8 to 1.8
- forces: float32 [3, 16, 8, 8, 512], P(None, 'gx', 'gy', 'gz'), may hold values from -6 to 6
- charges: float32 [16, 8, 8, 512], P('gx', 'gy', 'gz'), may hold values from -4 to 4
- atom_types: int32 [16, 8, 8, 512], P('gx', 'gy', 'gz'), may hold values from 0 to 31
- tile_counts: int32 [16, 8, 8], P('gx', 'gy', 'gz'), may hold values from 1 to 4, as said below
- pair_epsilon: float32 [32], replicated, may hold values from 0.01 to 0.1
- pair_sigma: float32 [32], replicated, may hold values from 0.1 to 0.15
Outputs:
- final_positions: float32 [3, 16, 8, 8, 512], P(None, 'gx', 'gy', 'gz')
- final_velocities: float32 [3, 16, 8, 8, 512], P(None, 'gx', 'gy', 'gz')
- final_forces: float32 [3, 16, 8, 8, 512], P(None, 'gx', 'gy', 'gz')
Inputs may be any that keep to these rules, and one draw needn't show every extreme that they name: The live atoms of a box are its first 128 times tile_counts slots; some box has 4 live tiles in every draw.
All inputs are finite; a program needn't handle non-finite values.
Results may differ from a plain program's by a relative error of at most 0.0003.
Values sent between devices are 32-bit elements; how exact they have to be, the bound alone decides.
A program may use at most 32 MiB of HBM per device.

v0:
```python
import jax
import jax.numpy as jnp
from jax import lax
from jax.sharding import PartitionSpec as P

TILE = 128
STEPS = 2


COULOMB = 0.02
KAPPA = 2.0
SOFTEN = 0.0225
CUTOFF = 0.81
TIME_STEP = 0.05
HALF_STEP = 0.025
HALF_PLATE = ((1, 0), (1, 1), (0, 1), (-1, 1))


def padded(block, sides, width):
    for axis, dim in sides:
        count = lax.axis_size(axis)
        forward = [(i, i + 1) for i in range(count - 1)]
        forward.append((count - 1, 0))
        backward = [(target, source) for source, target in forward]
        low = lax.ppermute(
            lax.slice_in_dim(block, block.shape[dim] - width, None, axis=dim), axis, forward
        )
        high = lax.ppermute(lax.slice_in_dim(block, 0, width, axis=dim), axis, backward)
        block = jnp.concatenate([low, block, high], axis=dim)
    return block


def pair_energy(left_pos, right_pos, left_par, right_par, weight):
    diff = left_pos[:, :, None] - right_pos[:, None, :]
    distance = jnp.sum(diff * diff, axis=0)
    soft_sq = distance + SOFTEN
    soft = jnp.sqrt(soft_sq)
    coulomb = COULOMB * left_par[0][:, None] * right_par[0][None, :] * jnp.exp(-KAPPA * soft) / soft
    sigma = 0.5 * (left_par[2][:, None] + right_par[2][None, :])
    ratio = sigma * sigma / soft_sq
    cubed = ratio * ratio * ratio
    lennard = 4.0 * left_par[1][:, None] * right_par[1][None, :] * (cubed * cubed - cubed)
    switch = jnp.square(jnp.maximum(1.0 - distance / CUTOFF, 0.0))
    return jnp.sum(weight * (coulomb + lennard) * switch)


def tile_pair(left, right, weight):

    def energy(left_pos, right_pos):
        return pair_energy(left_pos, right_pos, left[3:], right[3:], weight)

    value, pull = jax.vjp(energy, left[:3], right[:3])
    grad_left, grad_right = pull(jnp.ones_like(value))
    return (-grad_left, -grad_right)


def padded_forces(left, right, halve):
    tiles = left.shape[1] // TILE
    width = right.shape[1]
    pieces = left.reshape(6, tiles, TILE).transpose(1, 0, 2)
    starts = jnp.arange(tiles, dtype=jnp.int32) * TILE

    def visit(carry, item):
        piece, start = item
        if halve:
            rows = start + lax.broadcasted_iota(jnp.int32, (TILE, width), 0)
            cols = lax.broadcasted_iota(jnp.int32, (TILE, width), 1)
            weight = jnp.where(rows != cols, 0.5, 0.0).astype(left.dtype)
        else:
            weight = jnp.ones((), left.dtype)
        force_left, force_right = tile_pair(piece, right, weight)
        return (carry + force_right, force_left)

    force_right, stacked = lax.scan(visit, jnp.zeros((3, width), left.dtype), (pieces, starts))
    return (stacked.transpose(1, 0, 2).reshape(3, tiles * TILE), force_right)


def pair_forces(left, right):
    return padded_forces(left, right, False)


def move(record, along_x, along_y, along_z):
    shift = jnp.array([along_x, along_y, along_z], dtype=record.dtype)[:, None]
    return jnp.concatenate([record[:3] + shift, record[3:]], 0)


def one_side(places, params):
    slots = places.shape[1]
    record = jnp.concatenate([places, params], 0)
    cell = record.reshape(6, 1, 1, 1, slots)
    extended = padded(cell, (("gx", 1), ("gy", 2), ("gz", 3)), 1)
    below = extended[:, 1, 1, 0]
    above = extended[:, 1, 1, 2]
    plates = [extended[:, 1 + along_x, 1 + along_y, 1] for along_x, along_y in HALF_PLATE]
    above = move(above, 0, 0, 1)
    tower = jnp.concatenate([move(below, 0, 0, -1), record, above], 1)
    plate = jnp.concatenate(
        [move(member, offset[0], offset[1], 0) for member, offset in zip(plates, HALF_PLATE)], 1
    )
    force_tower, force_plate = pair_forces(tower, plate)
    force_above, force_own = pair_forces(above, record)
    self_left, self_right = padded_forces(record, record, True)
    own = force_tower[:, slots : 2 * slots] + force_own + self_left + self_right
    downward = force_tower[:, :slots]
    upward = force_tower[:, 2 * slots :] + force_above
    shell_buffer = jnp.zeros((3, 3, 3, 3, slots), places.dtype)
    shell_buffer = shell_buffer.at[:, 1, 1, 1].set(own)
    shell_buffer = shell_buffer.at[:, 1, 1, 0].set(downward)
    shell_buffer = shell_buffer.at[:, 1, 1, 2].set(upward)
    for number, (along_x, along_y) in enumerate(HALF_PLATE):
        part = force_plate[:, number * slots : (number + 1) * slots]
        shell_buffer = shell_buffer.at[:, 1 + along_x, 1 + along_y, 1].set(part)
    returned = padded(shell_buffer, (("gx", 1), ("gy", 2), ("gz", 3)), 1)
    total = jnp.sum(returned[:, 0::2, 0::2, 0::2], axis=(1, 2, 3))
    return total


def total_forces(places, params):
    return one_side(places, params)


def on_device(
    positions, velocities, forces, charges, atom_types, tile_counts, pair_epsilon, pair_sigma
):
    slots = positions.shape[-1]
    places = positions.reshape(3, slots)
    velocity = velocities.reshape(3, slots)
    pushing = forces.reshape(3, slots)
    index = lax.broadcasted_iota(jnp.int32, (slots,), 0)
    live = (index < tile_counts.reshape(()) * TILE).astype(places.dtype)
    kinds = lax.broadcasted_iota(jnp.int32, (pair_epsilon.shape[0], slots), 0)
    member = (atom_types.reshape(1, slots) == kinds).astype(places.dtype)
    root = jnp.sum(member * jnp.sqrt(pair_epsilon)[:, None], 0) * live
    sigma = jnp.sum(member * pair_sigma[:, None], 0)
    params = jnp.stack([charges.reshape(slots) * live, root, sigma], 0)
    for step in range(STEPS):
        velocity = velocity + HALF_STEP * pushing
        places = places + TIME_STEP * velocity
        pushing = total_forces(places, params)
        velocity = velocity + HALF_STEP * pushing
    shape = (3, 1, 1, 1, slots)
    return (places.reshape(shape), velocity.reshape(shape), pushing.reshape(shape))


def solution(mesh):
    in_specs = (
        P(None, "gx", "gy", "gz", None),
        P(None, "gx", "gy", "gz", None),
        P(None, "gx", "gy", "gz", None),
        P("gx", "gy", "gz", None),
        P("gx", "gy", "gz", None),
        P("gx", "gy", "gz"),
        P(),
        P(),
    )
    out_specs = (
        P(None, "gx", "gy", "gz", None),
        P(None, "gx", "gy", "gz", None),
        P(None, "gx", "gy", "gz", None),
    )
    return jax.shard_map(
        on_device, mesh=mesh, in_specs=in_specs, out_specs=out_specs, check_vma=False
    )
```

profile of v0, /device:TPU:6, one launch (start us, length us, event | category | flops | bytes accessed | tf_op | source)
XLA Modules:
  0.0 272.0 jit_solution(16226851620529366397)
XLA Ops:
  4.9 8.9 %collective-permute-start.1 = (f32[6,1,1,1,512]{4,0,3,2,1:T(8,128)S(1)}, f32[6,1,1,1,512]{4,0,3,2,1:T(8,128)S(1)}, u32[]{:S(2)}, u32[]{:S(2)}) collective-permute-start(f32[6,1,1,1,512]{4,0,3,2,1:T(8,128)S(1)} %fusion.154), channel_id=1, source_target_pairs={{64,0},{128,64},{192,128},{256,192},{320,256},{384,320},{448,384},... | collective-permute-start | bytes 36872 | tf_op jit(solution)/shard_map/ppermute | solution.py:28
  17.2 10.2 %while.94 = (s32[]{:T(128)}, f32[3,512]{1,0:T(4,128)S(1)}, f32[4,3,128]{2,1,0:T(4,128)S(1)}, f32[4,6,128]{2,0,1:T(4,128)S(1)}, f32[3,512]{1,0:T(4,128)S(1)}, /*i...) while((s32[]{:T(128)}, f32[3,512]{1,0:T(4,128)S(1)}, ...), condition=%wide.region_16.17_spmd.clone, body=%wide.region_12.16_spmd.clone.sunk | while | flops 5572486 | bytes 1112287 | solution.py:74
  29.9 4.6 %collective-permute-start.2 = (f32[6,3,1,1,512]{4,0,3,2,1:T(8,128)S(1)}, f32[6,3,1,1,512]{4,0,3,2,1:T(8,128)S(1)}, u32[]{:S(2)}, u32[]{:S(2)}) collective-permute-start(f32[6,3,1,1,512]{4,0,3,2,1:T(8,128)S(1)} %pad_maximum_fusion.26), channel_id=1, source_target_pairs={{0,8},{8,16},{16,24},{24,32},{32,40},{40,48},{48,56},{56,0},{1,9},... | collective-permute-start | bytes 110600 | tf_op jit(solution)/shard_map/ppermute | solution.py:25
  36.3 13.5 %collective-permute-start.5 = (f32[6,3,3,1,512]{4,0,3,2,1:T(8,128)S(1)}, f32[6,3,3,1,512]{4,0,3,2,1:T(8,128)S(1)}, u32[]{:S(2)}, u32[]{:S(2)}) collective-permute-start(f32[6,3,3,1,512]{4,0,3,2,1:T(8,128)S(1)} %pad_maximum_fusion.12), channel_id=1, source_target_pairs={{1,0},{2,1},{3,2},{4,3},{5,4},{6,5},{7,6},{0,7},{9,8},{10,9},{11,1... | collective-permute-start | bytes 331784 | tf_op jit(solution)/shard_map/ppermute | solution.py:28
  52.5 5.8 %collective-permute-done.4 = f32[6,3,3,1,512]{4,0,3,2,1:T(8,128)S(1)} collective-permute-done((f32[6,3,3,1,512]{4,0,3,2,1:T(8,128)S(1)}, f32[6,3,3,1,512]{4,0,3,2,1:T(8,128)S(1)}, u32[]{:S(2)}, u32[]{:S(2)}) %collective-permute-start.4) | collective-permute-done | bytes 110624 | tf_op jit(solution)/shard_map/ppermute | solution.py:25
  58.5 44.8 %while.92 = (s32[]{:T(128)}, f32[3,2048]{1,0:T(4,128)S(1)}, f32[12,3,128]{2,1,0:T(4,128)S(1)}, f32[12,6,128]{2,1,0:T(8,128)S(1)}, f32[6,2048]{1,0:T(8,128)S(1)}, /*index=5*/s32[]{:T(128)}, s32[]{:T(128)}) while((s32[]{:T(128)}, f32[3,2048]{1,0:T(4,128)S(1)}, f32[12,3,128]{2,1,0:T(4,128)S(1)}, f32[12,6,128]{2,1,0:T(8,128)S(1)}, ...), condition=%wide.region_6.0_spmd.clone, body=%wide.region_2.6_spmd.clone.sunk | while | flops 21240064 | bytes 4487263 | solution.py:74
  59.0 2.4 fusion.219
  62.7 2.4 fusion.219
  66.4 2.4 fusion.219
  70.2 2.4 fusion.219
  96.3 2.4 fusion.219
  100.0 2.4 fusion.219
  103.4 5.2 %while.93 = (s32[]{:T(128)}, f32[3,512]{1,0:T(4,128)S(1)}, f32[4,3,128]{2,1,0:T(4,128)S(1)}, f32[4,6,128]{2,0,1:T(4,128)S(1)}, f32[3,512]{1,0:T(4,128)S(1)}, /*i...) while((s32[]{:T(128)}, f32[3,512]{1,0:T(4,128)S(1)}, ...), condition=%wide.region_11.12_spmd.clone, body=%wide.region_7.11_spmd.clone.sunk | while | flops 5310214 | bytes 1111239 | solution.py:74
  110.7 6.0 %collective-permute-start.7 = (f32[3,1,3,3,512]{4,0,3,2,1:T(4,128)S(1)}, f32[3,1,3,3,512]{4,0,3,2,1:T(4,128)S(1)}, u32[]{:S(2)}, u32[]{:S(2)}) collective-permute-start(f32[3,1,3,3,512]{4,0,3,2,1:T(4,128)S(1)} %get-tuple-element.772), channel_id=1, source_target_pairs={{64,0},{128,64},{192,128},{256,192},{320,256},{384,320},{448,384},... | collective-permute-start | bytes 165896 | tf_op jit(solution)/shard_map/ppermute | solution.py:28
  118.8 5.2 %collective-permute-start.8 = (f32[3,5,1,3,512]{4,0,3,2,1:T(4,128)S(1)}, f32[3,5,1,3,512]{4,0,3,2,1:T(4,128)S(1)}, u32[]{:S(2)}, u32[]{:S(2)}) collective-permute-start(f32[3,5,1,3,512]{4,0,3,2,1:T(4,128)S(1)} %get-tuple-element.767), channel_id=1, source_target_pairs={{0,8},{8,16},{16,24},{24,32},{32,40},{40,48},{48,56},{56,0},{1,9},... | collective-permute-start | bytes 276488 | tf_op jit(solution)/shard_map/ppermute | solution.py:25
  126.4 5.6 %collective-permute-done.9 = f32[3,5,1,3,512]{4,0,3,2,1:T(4,128)S(1)} collective-permute-done((f32[3,5,1,3,512]{4,0,3,2,1:T(4,128)S(1)}, f32[3,5,1,3,512]{4,0,3,2,1:T(4,128)S(1)}, u32[]{:S(2)}, u32[]{:S(2)}) %collective-permute-start.9) | collective-permute-done | bytes 92192 | tf_op jit(solution)/shard_map/ppermute | solution.py:28
  134.0 5.8 %collective-permute-start.11 = (f32[3,5,5,1,512]{4,0,3,2,1:T(4,128)S(1)}, f32[3,5,5,1,512]{4,0,3,2,1:T(4,128)S(1)}, u32[]{:S(2)}, u32[]{:S(2)}) collective-permute-start(f32[3,5,5,1,512]{4,0,3,2,1:T(4,128)S(1)} %get-tuple-element.764), channel_id=1, source_target_pairs={{1,0},{2,1},{3,2},{4,3},{5,4},{6,5},{7,6},{0,7},{9,8},{10,9},{11,1... | collective-permute-start | bytes 460808 | tf_op jit(solution)/shard_map/ppermute | solution.py:28
  145.6 6.2 %collective-permute-start.13 = (f32[6,1,1,1,512]{4,0,3,2,1:T(8,128)S(1)}, f32[6,1,1,1,512]{4,0,3,2,1:T(8,128)S(1)}, u32[]{:S(2)}, u32[]{:S(2)}) collective-permute-start(f32[6,1,1,1,512]{4,0,3,2,1:T(8,128)S(1)} %fusion.155), channel_id=1, source_target_pairs={{64,0},{128,64},{192,128},{256,192},{320,256},{384,320},{448,384},... | collective-permute-start | bytes 36872 | tf_op jit(solution)/shard_map/ppermute | solution.py:28
  151.9 10.3 %while.97 = (s32[]{:T(128)}, f32[3,512]{1,0:T(4,128)S(1)}, f32[4,3,128]{2,1,0:T(4,128)S(1)}, f32[4,6,128]{2,0,1:T(4,128)S(1)}, f32[3,512]{1,0:T(4,128)S(1)}, /*i...) while((s32[]{:T(128)}, f32[3,512]{1,0:T(4,128)S(1)}, ...), condition=%wide.region_32.33_spmd.clone, body=%wide.region_28.32_spmd.clone.sunk | while | flops 5572486 | bytes 1112287 | solution.py:74
  164.1 5.1 %collective-permute-start.14 = (f32[6,3,1,1,512]{4,0,3,2,1:T(8,128)S(1)}, f32[6,3,1,1,512]{4,0,3,2,1:T(8,128)S(1)}, u32[]{:S(2)}, u32[]{:S(2)}) collective-permute-start(f32[6,3,1,1,512]{4,0,3,2,1:T(8,128)S(1)} %pad_maximum_fusion.27), channel_id=1, source_target_pairs={{0,8},{8,16},{16,24},{24,32},{32,40},{40,48},{48,56},{56,0},{1,9},... | collective-permute-start | bytes 110600 | tf_op jit(solution)/shard_map/ppermute | solution.py:25
  171.0 4.5 %collective-permute-start.17 = (f32[6,3,3,1,512]{4,0,3,2,1:T(8,128)S(1)}, f32[6,3,3,1,512]{4,0,3,2,1:T(8,128)S(1)}, u32[]{:S(2)}, u32[]{:S(2)}) collective-permute-start(f32[6,3,3,1,512]{4,0,3,2,1:T(8,128)S(1)} %pad_maximum_fusion.13), channel_id=1, source_target_pairs={{1,0},{2,1},{3,2},{4,3},{5,4},{6,5},{7,6},{0,7},{9,8},{10,9},{11,1... | collective-permute-start | bytes 331784 | tf_op jit(solution)/shard_map/ppermute | solution.py:28
  178.3 5.8 %collective-permute-done.16 = f32[6,3,3,1,512]{4,0,3,2,1:T(8,128)S(1)} collective-permute-done((f32[6,3,3,1,512]{4,0,3,2,1:T(8,128)S(1)}, f32[6,3,3,1,512]{4,0,3,2,1:T(8,128)S(1)}, u32[]{:S(2)}, u32[]{:S(2)}) %collective-permute-start.16) | collective-permute-done | bytes 110624 | tf_op jit(solution)/shard_map/ppermute | solution.py:25
  184.2 44.8 %while.95 = (s32[]{:T(128)}, f32[3,2048]{1,0:T(4,128)S(1)}, f32[12,3,128]{2,1,0:T(4,128)S(1)}, f32[12,6,128]{2,1,0:T(8,128)S(1)}, f32[6,2048]{1,0:T(8,128)S(1)}, /*index=5*/s32[]{:T(128)}, s32[]{:T(128)}) while((s32[]{:T(128)}, f32[3,2048]{1,0:T(4,128)S(1)}, f32[12,3,128]{2,1,0:T(4,128)S(1)}, f32[12,6,128]{2,1,0:T(8,128)S(1)}, ...), condition=%wide.region_22.23_spmd.clone, body=%wide.region_18.22_spmd.clone.sunk | while | flops 21240064 | bytes 4487263 | solution.py:74
  195.9 2.4 fusion.233
  199.6 2.4 fusion.233
  203.4 2.4 fusion.233
  229.1 5.2 %while.96 = (s32[]{:T(128)}, f32[3,512]{1,0:T(4,128)S(1)}, f32[4,3,128]{2,1,0:T(4,128)S(1)}, f32[4,6,128]{2,0,1:T(4,128)S(1)}, f32[3,512]{1,0:T(4,128)S(1)}, /*i...) while((s32[]{:T(128)}, f32[3,512]{1,0:T(4,128)S(1)}, ...), condition=%wide.region_27.28_spmd.clone, body=%wide.region_23.27_spmd.clone.sunk | while | flops 5310214 | bytes 1111239 | solution.py:74
  236.4 6.0 %collective-permute-start.19 = (f32[3,1,3,3,512]{4,0,3,2,1:T(4,128)S(1)}, f32[3,1,3,3,512]{4,0,3,2,1:T(4,128)S(1)}, u32[]{:S(2)}, u32[]{:S(2)}) collective-permute-start(f32[3,1,3,3,512]{4,0,3,2,1:T(4,128)S(1)} %get-tuple-element.770), channel_id=1, source_target_pairs={{64,0},{128,64},{192,128},{256,192},{320,256},{384,320},{448,384},... | collective-permute-start | bytes 165896 | tf_op jit(solution)/shard_map/ppermute | solution.py:28
  244.5 5.2 %collective-permute-start.20 = (f32[3,5,1,3,512]{4,0,3,2,1:T(4,128)S(1)}, f32[3,5,1,3,512]{4,0,3,2,1:T(4,128)S(1)}, u32[]{:S(2)}, u32[]{:S(2)}) collective-permute-start(f32[3,5,1,3,512]{4,0,3,2,1:T(4,128)S(1)} %get-tuple-element.765), channel_id=1, source_target_pairs={{0,8},{8,16},{16,24},{24,32},{32,40},{40,48},{48,56},{56,0},{1,9},... | collective-permute-start | bytes 276488 | tf_op jit(solution)/shard_map/ppermute | solution.py:25
  252.1 5.6 %collective-permute-done.21 = f32[3,5,1,3,512]{4,0,3,2,1:T(4,128)S(1)} collective-permute-done((f32[3,5,1,3,512]{4,0,3,2,1:T(4,128)S(1)}, f32[3,5,1,3,512]{4,0,3,2,1:T(4,128)S(1)}, u32[]{:S(2)}, u32[]{:S(2)}) %collective-permute-start.21) | collective-permute-done | bytes 92192 | tf_op jit(solution)/shard_map/ppermute | solution.py:28
  259.7 5.8 %collective-permute-start.23 = (f32[3,5,5,1,512]{4,0,3,2,1:T(4,128)S(1)}, f32[3,5,5,1,512]{4,0,3,2,1:T(4,128)S(1)}, u32[]{:S(2)}, u32[]{:S(2)}) collective-permute-start(f32[3,5,5,1,512]{4,0,3,2,1:T(4,128)S(1)} %get-tuple-element.762), channel_id=1, source_target_pairs={{1,0},{2,1},{3,2},{4,3},{5,4},{6,5},{7,6},{0,7},{9,8},{10,9},{11,1... | collective-permute-start | bytes 460808 | tf_op jit(solution)/shard_map/ppermute | solution.py:28
  267.1 3.4 %collective-permute-done.23 = f32[3,5,5,1,512]{4,0,3,2,1:T(4,128)S(1)} collective-permute-done((f32[3,5,5,1,512]{4,0,3,2,1:T(4,128)S(1)}, f32[3,5,5,1,512]{4,0,3,2,1:T(4,128)S(1)}, u32[]{:S(2)}, u32[]{:S(2)}) %collective-permute-start.23) | collective-permute-done | bytes 153632 | tf_op jit(solution)/shard_map/ppermute | solution.py:28
  (524 shorter events, 142.1 us)
Async XLA Ops:
  4.9 22.6 %collective-permute-start.1 = (f32[6,1,1,1,512]{4,0,3,2,1:T(8,128)S(1)}, f32[6,1,1,1,512]{4,0,3,2,1:T(8,128)S(1)}, u32[]{:S(2)}, u32[]{:S(2)}) collective-permute-start(f32[6,1,1,1,512]{4,0,3,2,1:T(8,128)S(1)} %fusion.154), channel_id=1, source_target_pairs={{64,0},{128,64},{192,128},{256,192},{320,256},{384,320},{448,384},... | collective-permute-start | bytes 36872 | tf_op jit(solution)/shard_map/ppermute | solution.py:28
  13.8 13.7 %collective-permute-start = (f32[6,1,1,1,512]{4,0,3,2,1:T(8,128)S(1)}, f32[6,1,1,1,512]{4,0,3,2,1:T(8,128)S(1)}, u32[]{:S(2)}, u32[]{:S(2)}) collective-permute-start(f32[6,1,1,1,512]{4,0,3,2,1:T(8,128)S(1)} %fusion.154), channel_id=1, source_target_pairs={{0,64},{64,128},{128,192},{192,256},{256,320},{320,384},{384,448},... | collective-permute-start | bytes 36872 | tf_op jit(solution)/shard_map/ppermute | solution.py:25
  17.1 17.4 %copy-start.6 = (f32[3]{0:T(128)S(1)}, f32[3]{0:T(128)}, u32[]{:S(2)}) copy-start(f32[3]{0:T(128)} %constant.589.clone) | copy-start | bytes 40
  17.1 34.6 %copy-start.2 = (f32[3]{0:T(128)S(1)}, f32[3]{0:T(128)}, u32[]{:S(2)}) copy-start(f32[3]{0:T(128)} %constant.590.clone) | copy-start | bytes 40
  17.1 34.6 %copy-start.3 = (f32[3]{0:T(128)S(1)}, f32[3]{0:T(128)}, u32[]{:S(2)}) copy-start(f32[3]{0:T(128)} %constant.591.clone) | copy-start | bytes 40
  17.2 34.6 %copy-start.4 = (f32[3]{0:T(128)S(1)}, f32[3]{0:T(128)}, u32[]{:S(2)}) copy-start(f32[3]{0:T(128)} %constant.592.clone) | copy-start | bytes 40
  17.2 35.3 %copy-start.1 = (f32[3]{0:T(128)S(1)}, f32[3]{0:T(128)}, u32[]{:S(2)}) copy-start(f32[3]{0:T(128)} %constant.587.clone) | copy-start | bytes 40
  17.2 41.2 %copy-start.5 = (f32[3]{0:T(128)S(1)}, f32[3]{0:T(128)}, u32[]{:S(2)}) copy-start(f32[3]{0:T(128)} %constant.588.clone) | copy-start | bytes 40
  27.4 7.2 %collective-permute-start.3 = (f32[6,3,1,1,512]{4,0,3,2,1:T(8,128)S(1)}, f32[6,3,1,1,512]{4,0,3,2,1:T(8,128)S(1)}, u32[]{:S(2)}, u32[]{:S(2)}) collective-permute-start(f32[6,3,1,1,512]{4,0,3,2,1:T(8,128)S(1)} %pad_maximum_fusion.26), channel_id=1, source_target_pairs={{8,0},{16,8},{24,16},{32,24},{40,32},{48,40},{56,48},{0,56},{9,1},... | collective-permute-start | bytes 110600 | tf_op jit(solution)/shard_map/ppermute | solution.py:28
  29.9 6.3 %collective-permute-start.2 = (f32[6,3,1,1,512]{4,0,3,2,1:T(8,128)S(1)}, f32[6,3,1,1,512]{4,0,3,2,1:T(8,128)S(1)}, u32[]{:S(2)}, u32[]{:S(2)}) collective-permute-start(f32[6,3,1,1,512]{4,0,3,2,1:T(8,128)S(1)} %pad_maximum_fusion.26), channel_id=1, source_target_pairs={{0,8},{8,16},{16,24},{24,32},{32,40},{40,48},{48,56},{56,0},{1,9},... | collective-permute-start | bytes 110600 | tf_op jit(solution)/shard_map/ppermute | solution.py:25
  36.3 16.2 %collective-permute-start.5 = (f32[6,3,3,1,512]{4,0,3,2,1:T(8,128)S(1)}, f32[6,3,3,1,512]{4,0,3,2,1:T(8,128)S(1)}, u32[]{:S(2)}, u32[]{:S(2)}) collective-permute-start(f32[6,3,3,1,512]{4,0,3,2,1:T(8,128)S(1)} %pad_maximum_fusion.12), channel_id=1, source_target_pairs={{1,0},{2,1},{3,2},{4,3},{5,4},{6,5},{7,6},{0,7},{9,8},{10,9},{11,1... | collective-permute-start | bytes 331784 | tf_op jit(solution)/shard_map/ppermute | solution.py:28
  49.8 8.6 %collective-permute-start.4 = (f32[6,3,3,1,512]{4,0,3,2,1:T(8,128)S(1)}, f32[6,3,3,1,512]{4,0,3,2,1:T(8,128)S(1)}, u32[]{:S(2)}, u32[]{:S(2)}) collective-permute-start(f32[6,3,3,1,512]{4,0,3,2,1:T(8,128)S(1)} %pad_maximum_fusion.12), channel_id=1, source_target_pairs={{0,1},{1,2},{2,3},{3,4},{4,5},{5,6},{6,7},{7,0},{8,9},{9,10},{10,1... | collective-permute-start | bytes 331784 | tf_op jit(solution)/shard_map/ppermute | solution.py:25
  108.8 8.5 %collective-permute-start.6 = (f32[3,1,3,3,512]{4,0,3,2,1:T(4,128)S(1)}, f32[3,1,3,3,512]{4,0,3,2,1:T(4,128)S(1)}, u32[]{:S(2)}, u32[]{:S(2)}) collective-permute-start(f32[3,1,3,3,512]{4,0,3,2,1:T(4,128)S(1)} %get-tuple-element.771), channel_id=1, source_target_pairs={{0,64},{64,128},{128,192},{192,256},{256,320},{320,384},{384,448},... | collective-permute-start | bytes 165896 | tf_op jit(solution)/shard_map/ppermute | solution.py:25
  110.7 8.0 %collective-permute-start.7 = (f32[3,1,3,3,512]{4,0,3,2,1:T(4,128)S(1)}, f32[3,1,3,3,512]{4,0,3,2,1:T(4,128)S(1)}, u32[]{:S(2)}, u32[]{:S(2)}) collective-permute-start(f32[3,1,3,3,512]{4,0,3,2,1:T(4,128)S(1)} %get-tuple-element.772), channel_id=1, source_target_pairs={{64,0},{128,64},{192,128},{256,192},{320,256},{384,320},{448,384},... | collective-permute-start | bytes 165896 | tf_op jit(solution)/shard_map/ppermute | solution.py:28
  118.8 7.6 %collective-permute-start.8 = (f32[3,5,1,3,512]{4,0,3,2,1:T(4,128)S(1)}, f32[3,5,1,3,512]{4,0,3,2,1:T(4,128)S(1)}, u32[]{:S(2)}, u32[]{:S(2)}) collective-permute-start(f32[3,5,1,3,512]{4,0,3,2,1:T(4,128)S(1)} %get-tuple-element.767), channel_id=1, source_target_pairs={{0,8},{8,16},{16,24},{24,32},{32,40},{40,48},{48,56},{56,0},{1,9},... | collective-permute-start | bytes 276488 | tf_op jit(solution)/shard_map/ppermute | solution.py:25
  123.9 8.0 %collective-permute-start.9 = (f32[3,5,1,3,512]{4,0,3,2,1:T(4,128)S(1)}, f32[3,5,1,3,512]{4,0,3,2,1:T(4,128)S(1)}, u32[]{:S(2)}, u32[]{:S(2)}) collective-permute-start(f32[3,5,1,3,512]{4,0,3,2,1:T(4,128)S(1)} %get-tuple-element.768), channel_id=1, source_target_pairs={{8,0},{16,8},{24,16},{32,24},{40,32},{48,40},{56,48},{0,56},{9,1},... | collective-permute-start | bytes 276488 | tf_op jit(solution)/shard_map/ppermute | solution.py:28
  132.0 9.4 %collective-permute-start.10 = (f32[3,5,5,1,512]{4,0,3,2,1:T(4,128)S(1)}, f32[3,5,5,1,512]{4,0,3,2,1:T(4,128)S(1)}, u32[]{:S(2)}, u32[]{:S(2)}) collective-permute-start(f32[3,5,5,1,512]{4,0,3,2,1:T(4,128)S(1)} %get-tuple-element.763), channel_id=1, source_target_pairs={{0,1},{1,2},{2,3},{3,4},{4,5},{5,6},{6,7},{7,0},{8,9},{9,10},{10,1... | collective-permute-start | bytes 460808 | tf_op jit(solution)/shard_map/ppermute | solution.py:25
  134.0 9.4 %collective-permute-start.11 = (f32[3,5,5,1,512]{4,0,3,2,1:T(4,128)S(1)}, f32[3,5,5,1,512]{4,0,3,2,1:T(4,128)S(1)}, u32[]{:S(2)}, u32[]{:S(2)}) collective-permute-start(f32[3,5,5,1,512]{4,0,3,2,1:T(4,128)S(1)} %get-tuple-element.764), channel_id=1, source_target_pairs={{1,0},{2,1},{3,2},{4,3},{5,4},{6,5},{7,6},{0,7},{9,8},{10,9},{11,1... | collective-permute-start | bytes 460808 | tf_op jit(solution)/shard_map/ppermute | solution.py:28
  139.7 3.9 %copy-start = (f32[3,1,1,1,512]{4,3,2,1,0:T(1,128)S(1)}, f32[3,1,1,1,512]{4,3,2,1,0:T(1,128)}, u32[]{:S(2)}) copy-start(f32[3,1,1,1,512]{4,3,2,1,0:T(1,128)} %param.60) | copy-start | bytes 18436
  143.7 18.5 %collective-permute-start.12 = (f32[6,1,1,1,512]{4,0,3,2,1:T(8,128)S(1)}, f32[6,1,1,1,512]{4,0,3,2,1:T(8,128)S(1)}, u32[]{:S(2)}, u32[]{:S(2)}) collective-permute-start(f32[6,1,1,1,512]{4,0,3,2,1:T(8,128)S(1)} %fusion.155), channel_id=1, source_target_pairs={{0,64},{64,128},{128,192},{192,256},{256,320},{320,384},{384,448},... | collective-permute-start | bytes 36872 | tf_op jit(solution)/shard_map/ppermute | solution.py:25
  145.6 16.6 %collective-permute-start.13 = (f32[6,1,1,1,512]{4,0,3,2,1:T(8,128)S(1)}, f32[6,1,1,1,512]{4,0,3,2,1:T(8,128)S(1)}, u32[]{:S(2)}, u32[]{:S(2)}) collective-permute-start(f32[6,1,1,1,512]{4,0,3,2,1:T(8,128)S(1)} %fusion.155), channel_id=1, source_target_pairs={{64,0},{128,64},{192,128},{256,192},{320,256},{384,320},{448,384},... | collective-permute-start | bytes 36872 | tf_op jit(solution)/shard_map/ppermute | solution.py:28
  162.2 7.2 %collective-permute-start.15 = (f32[6,3,1,1,512]{4,0,3,2,1:T(8,128)S(1)}, f32[6,3,1,1,512]{4,0,3,2,1:T(8,128)S(1)}, u32[]{:S(2)}, u32[]{:S(2)}) collective-permute-start(f32[6,3,1,1,512]{4,0,3,2,1:T(8,128)S(1)} %pad_maximum_fusion.27), channel_id=1, source_target_pairs={{8,0},{16,8},{24,16},{32,24},{40,32},{48,40},{56,48},{0,56},{9,1},... | collective-permute-start | bytes 110600 | tf_op jit(solution)/shard_map/ppermute | solution.py:28
  164.1 6.9 %collective-permute-start.14 = (f32[6,3,1,1,512]{4,0,3,2,1:T(8,128)S(1)}, f32[6,3,1,1,512]{4,0,3,2,1:T(8,128)S(1)}, u32[]{:S(2)}, u32[]{:S(2)}) collective-permute-start(f32[6,3,1,1,512]{4,0,3,2,1:T(8,128)S(1)} %pad_maximum_fusion.27), channel_id=1, source_target_pairs={{0,8},{8,16},{16,24},{24,32},{32,40},{40,48},{48,56},{56,0},{1,9},... | collective-permute-start | bytes 110600 | tf_op jit(solution)/shard_map/ppermute | solution.py:25
  171.0 7.2 %collective-permute-start.17 = (f32[6,3,3,1,512]{4,0,3,2,1:T(8,128)S(1)}, f32[6,3,3,1,512]{4,0,3,2,1:T(8,128)S(1)}, u32[]{:S(2)}, u32[]{:S(2)}) collective-permute-start(f32[6,3,3,1,512]{4,0,3,2,1:T(8,128)S(1)} %pad_maximum_fusion.13), channel_id=1, source_target_pairs={{1,0},{2,1},{3,2},{4,3},{5,4},{6,5},{7,6},{0,7},{9,8},{10,9},{11,1... | collective-permute-start | bytes 331784 | tf_op jit(solution)/shard_map/ppermute | solution.py:28
  175.5 8.6 %collective-permute-start.16 = (f32[6,3,3,1,512]{4,0,3,2,1:T(8,128)S(1)}, f32[6,3,3,1,512]{4,0,3,2,1:T(8,128)S(1)}, u32[]{:S(2)}, u32[]{:S(2)}) collective-permute-start(f32[6,3,3,1,512]{4,0,3,2,1:T(8,128)S(1)} %pad_maximum_fusion.13), channel_id=1, source_target_pairs={{0,1},{1,2},{2,3},{3,4},{4,5},{5,6},{6,7},{7,0},{8,9},{9,10},{10,1... | collective-permute-start | bytes 331784 | tf_op jit(solution)/shard_map/ppermute | solution.py:25
  234.5 8.5 %collective-permute-start.18 = (f32[3,1,3,3,512]{4,0,3,2,1:T(4,128)S(1)}, f32[3,1,3,3,512]{4,0,3,2,1:T(4,128)S(1)}, u32[]{:S(2)}, u32[]{:S(2)}) collective-permute-start(f32[3,1,3,3,512]{4,0,3,2,1:T(4,128)S(1)} %get-tuple-element.769), channel_id=1, source_target_pairs={{0,64},{64,128},{128,192},{192,256},{256,320},{320,384},{384,448},... | collective-permute-start | bytes 165896 | tf_op jit(solution)/shard_map/ppermute | solution.py:25
  236.4 8.0 %collective-permute-start.19 = (f32[3,1,3,3,512]{4,0,3,2,1:T(4,128)S(1)}, f32[3,1,3,3,512]{4,0,3,2,1:T(4,128)S(1)}, u32[]{:S(2)}, u32[]{:S(2)}) collective-permute-start(f32[3,1,3,3,512]{4,0,3,2,1:T(4,128)S(1)} %get-tuple-element.770), channel_id=1, source_target_pairs={{64,0},{128,64},{192,128},{256,192},{320,256},{384,320},{448,384},... | collective-permute-start | bytes 165896 | tf_op jit(solution)/shard_map/ppermute | solution.py:28
  244.5 7.6 %collective-permute-start.20 = (f32[3,5,1,3,512]{4,0,3,2,1:T(4,128)S(1)}, f32[3,5,1,3,512]{4,0,3,2,1:T(4,128)S(1)}, u32[]{:S(2)}, u32[]{:S(2)}) collective-permute-start(f32[3,5,1,3,512]{4,0,3,2,1:T(4,128)S(1)} %get-tuple-element.765), channel_id=1, source_target_pairs={{0,8},{8,16},{16,24},{24,32},{32,40},{40,48},{48,56},{56,0},{1,9},... | collective-permute-start | bytes 276488 | tf_op jit(solution)/shard_map/ppermute | solution.py:25
  249.7 8.0 %collective-permute-start.21 = (f32[3,5,1,3,512]{4,0,3,2,1:T(4,128)S(1)}, f32[3,5,1,3,512]{4,0,3,2,1:T(4,128)S(1)}, u32[]{:S(2)}, u32[]{:S(2)}) collective-permute-start(f32[3,5,1,3,512]{4,0,3,2,1:T(4,128)S(1)} %get-tuple-element.766), channel_id=1, source_target_pairs={{8,0},{16,8},{24,16},{32,24},{40,32},{48,40},{56,48},{0,56},{9,1},... | collective-permute-start | bytes 276488 | tf_op jit(solution)/shard_map/ppermute | solution.py:28
  257.8 9.3 %collective-permute-start.22 = (f32[3,5,5,1,512]{4,0,3,2,1:T(4,128)S(1)}, f32[3,5,5,1,512]{4,0,3,2,1:T(4,128)S(1)}, u32[]{:S(2)}, u32[]{:S(2)}) collective-permute-start(f32[3,5,5,1,512]{4,0,3,2,1:T(4,128)S(1)} %get-tuple-element.761), channel_id=1, source_target_pairs={{0,1},{1,2},{2,3},{3,4},{4,5},{5,6},{6,7},{7,0},{8,9},{9,10},{10,1... | collective-permute-start | bytes 460808 | tf_op jit(solution)/shard_map/ppermute | solution.py:25
  259.7 10.8 %collective-permute-start.23 = (f32[3,5,5,1,512]{4,0,3,2,1:T(4,128)S(1)}, f32[3,5,5,1,512]{4,0,3,2,1:T(4,128)S(1)}, u32[]{:S(2)}, u32[]{:S(2)}) collective-permute-start(f32[3,5,5,1,512]{4,0,3,2,1:T(4,128)S(1)} %get-tuple-element.762), channel_id=1, source_target_pairs={{1,0},{2,1},{3,2},{4,3},{5,4},{6,5},{7,6},{0,7},{9,8},{10,9},{11,1... | collective-permute-start | bytes 460808 | tf_op jit(solution)/shard_map/ppermute | solution.py:28
where the time goes:
time: 273 us; the launch traced here: 272 us
  other arithmetic  118 us (43%)
  starting transfers between devices  101 us (37%)
  waiting for transfers between devices  40.6 us (15%)
  local copies, waits for them, and re-layouts  7.8 us (3%)
  loops' own time  2.94 us (1%)
    add_any x40, other arithmetic, pair_energy(): soft = jnp.sqrt(soft_sq)  70.4 us
    ppermute x12, starting transfers between devices, padded(): lax.ppermute(lax.slice_in_dim(block, 0, width, axis=dim), axis, backward)  64.9 us
    ppermute x12, starting transfers between devices, padded(): lax.ppermute(lax.slice_in_dim(block, block.shape[dim] - width, None, axis...  35.6 us
    reduce_sum x40, other arithmetic, pair_energy(): diff = left_pos[:, :, None] - right_pos[:, None, :]  22.8 us
    ppermute x12, waiting for transfers between devices, padded(): lax.ppermute(lax.slice_in_dim(block, 0, width, axis=dim), axis, backward)  20.5 us
    ppermute x12, waiting for transfers between devices, padded(): lax.ppermute(lax.slice_in_dim(block, block.shape[dim] - width, None, axis...  20.1 us
    reduce_sum x40, other arithmetic, pair_energy(): distance = jnp.sum(diff * diff, axis=0)  11.3 us
  transfers between devices with their start and end apart: 24, of which 18 were waited for; matrix products, arithmetic and copies ran while one was open for 8% of the time, Pallas kernels for 0%

commit v1 on v0

v1 whole, which is shorter than its diff:
```python
import functools

import jax
import jax.numpy as jnp
from jax import lax
from jax.experimental import pallas as pl
from jax.experimental.pallas import tpu as pltpu
from jax.sharding import PartitionSpec as P

TILE = 128
STEPS = 2
TIME_STEP = 0.05
HALF_STEP = 0.025
PLATE = ((1, 0), (1, 1), (0, 1), (-1, 1))
NP = len(PLATE)
OFFSETS = tuple((x, y, 0) for x, y in PLATE) + ((0, 0, -1), (0, 0, 1))
NBR = NP + 2
AXES = ("gx", "gy", "gz")
MESH = pl.DeviceIdType.MESH
F32 = jnp.float32
BF16 = jnp.bfloat16
FAR = 1e6
RB = NP + 2
UN = 4
LOG2E = 1.4426950408889634
FORCE = 8.0 / (3.24 * 3.24)

def pair_kernel(joined, pos_ref, par_ref, own_ref, ownpar_ref, fout_ref, fown_ref,
                left, right, acc_left, list_v, list_s, sem):
    position = (lambda k: pos_ref[k, 0]) if joined else (lambda k: pos_ref[k])
    lane16 = lax.broadcasted_iota(jnp.int32, (1, 16), 1)
    row16 = lax.broadcasted_iota(jnp.int32, (16, 1), 0)
    for k in range(RB):
        if k < NP:
            p = position(k) + jnp.where(row16 < 4, float(PLATE[k][0]), jnp.where(row16 < 8, float(PLATE[k][1]), 0.0))
            a = par_ref[k, 1]
        else:
            p = own_ref[0] if joined else own_ref[...]
            a = ownpar_ref[1]
        p = p * 2.0
        for f in range(3):
            right[f, 4 * k:4 * k + 4, :] = p[4 * f:4 * f + 4]
            right[3 + f, 4 * k:4 * k + 4, :] = a[4 * f:4 * f + 4]
    mins, maxs = [], []
    qscale = jnp.where(lane16 < 4, 0.04 / 6.0 * FORCE, jnp.where(lane16 < 8, 4.0 * FORCE, 1.0))
    for box in range(3):
        if box == 1:
            p, a = (own_ref[0] if joined else own_ref[...]), ownpar_ref[1]
        else:
            slot = NP if box == 0 else NP + 1
            p = position(slot) + jnp.where((row16 >= 8) & (row16 < 12), -1.0 if box == 0 else 1.0, 0.0)
            a = par_ref[slot, 1]
        tp = jnp.transpose(jnp.concatenate([p * 2.0, a], 0), (1, 0))
        lo = tp[:, :16].reshape(4, 32, 16)
        mins.append(jnp.min(lo, axis=1))
        maxs.append(jnp.max(lo, axis=1))
        ta = tp[:, 16:] * qscale
        for t in range(4):
            base = (t * 16 + box * 4) * 4
            for f in range(6):
                col = tp[:, 4 * f + t:4 * f + t + 1] if f < 3 else ta[:, 4 * (f - 3) + t:4 * (f - 3) + t + 1]
                left[f, base:base + 16] = jnp.broadcast_to(col, (128, 128)).reshape(16, 8, 128)
    for f in range(6):
        left[f, 48:64] = jnp.full((16, 8, 128), FAR if f < 3 else 0.0, F32)
    acc_left[...] = jnp.zeros_like(acc_left)
    lmin = jnp.concatenate(mins + [jnp.full((4, 16), FAR, F32)], 0)
    lmax = jnp.concatenate(maxs + [jnp.full((4, 16), FAR, F32)], 0)
    rows = 4 * RB
    d2 = jnp.zeros((64, 128), F32)
    live = None
    for f in range(3):
        a0 = jnp.concatenate([lmin[:, 4 * f + t:4 * f + t + 1] for t in range(4)], 0)
        a1 = jnp.concatenate([lmax[:, 4 * f + t:4 * f + t + 1] for t in range(4)], 0)
        v = jnp.concatenate([right[f, :rows, :], jnp.full((128 - rows, 128), FAR, F32)], 0)
        b0 = jnp.transpose(jnp.broadcast_to(jnp.min(v, axis=1, keepdims=True), (128, 128)), (1, 0))[:1]
        b1 = jnp.transpose(jnp.broadcast_to(jnp.max(v, axis=1, keepdims=True), (128, 128)), (1, 0))[:1]
        gap = jnp.maximum(jnp.maximum(a0 - b1, b0 - a1), 0.0)
        d2 = d2 + gap * gap
        if f == 0:
            live = a0 < 0.1 * FAR
    row = lax.broadcasted_iota(jnp.int32, (64, 128), 0)
    col = lax.broadcasted_iota(jnp.int32, (64, 128), 1)
    lt, lbox = row // 16, (row // 4) % 4
    rbox, rt = col // 4, col % 4
    plate = (rbox < NP) & (lbox < 3)
    inner = (rbox == NP) & ((lbox == 2) | ((lbox == 1) & (lt < rt)))
    diag = (rbox == NP + 1) & (lbox == 1) & (lt == rt)
    m = (d2 < 3.2401) & live & (plate | inner | diag)
    mf = m.astype(BF16)
    r64 = lax.broadcasted_iota(jnp.int32, (64, 64), 0)
    c64 = lax.broadcasted_iota(jnp.int32, (64, 64), 1)
    before = jnp.dot((c64 < r64).astype(BF16), mf, preferred_element_type=F32)
    place = jnp.where(m, before.astype(jnp.int32), -1)
    count = jnp.sum(m.astype(jnp.int32), axis=0, keepdims=True)
    value = row - 12
    for k in range(48):
        list_v[k:k + 1, :] = jnp.sum(jnp.where(place == k, value, 0), axis=0, keepdims=True) + 12
    list_v[48:49, :] = count
    copy = pltpu.make_async_copy(list_v, list_s, sem)
    copy.start()
    copy.wait()

    def one_tile(r, _):
        trips = (list_s[48, r] + (UN - 1)) // UN
        rx, ry, rz, rq, re, rs_ = [jnp.broadcast_to(right[f, pl.ds(r, 1), :], (8, 128))[None] for f in range(6)]

        def body(it, acc):
            ax, ay, az = acc
            for j in range(UN):
                b = list_s[it * UN + j, r] * 4
                dx = left[0, pl.ds(b, 4)] - rx
                dy = left[1, pl.ds(b, 4)] - ry
                dz = left[2, pl.ds(b, 4)] - rz
                s2 = (dx * dx + 0.09) + dy * dy + dz * dz
                rs = lax.rsqrt(s2)
                inv = rs * rs
                ex = jnp.exp2(s2 * (-LOG2E) * rs)
                w = jnp.maximum(3.33 - s2, 0.0)
                bb = (w * inv) * 1.5
                a2 = bb + 1.0
                a1 = a2 + bb
                sg = left[5, pl.ds(b, 4)] + rs_
                tt = sg * sg * inv
                t3 = tt * tt * tt
                ll = (left[4, pl.ds(b, 4)] * re) * t3
                lj = ll * (t3 * a1 - a2)
                cc = (left[3, pl.ds(b, 4)] * rq) * ex * (rs * (a2 + 5.0) + bb)
                g = (lj + cc) * w
                fx, fy, fz = g * dx, g * dy, g * dz
                acc_left[0, pl.ds(b, 4)] += fx
                acc_left[1, pl.ds(b, 4)] += fy
                acc_left[2, pl.ds(b, 4)] += fz
                ax = ax - jnp.sum(fx, axis=0)
                ay = ay - jnp.sum(fy, axis=0)
                az = az - jnp.sum(fz, axis=0)
            return ax, ay, az

        zero = jnp.zeros((8, 128), F32)
        acc = lax.fori_loop(0, trips, body, (zero, zero, zero))
        for f in range(3):
            right[f, pl.ds(r, 1), :] = jnp.sum(acc[f], axis=0, keepdims=True)
        return 0

    lax.fori_loop(0, rows, one_tile, 0)
    zero4 = jnp.zeros((4, 128), F32)
    for k in range(NP):
        fout_ref[k] = jnp.concatenate([right[f, 4 * k:4 * k + 4, :] for f in range(3)] + [zero4], 0)
    ones = jnp.ones((8, 128), BF16)
    for box in range(3):
        out = []
        for f in range(3):
            for t in range(4):
                base = (t * 16 + box * 4) * 4
                a = acc_left[f, base:base + 16].reshape(128, 128)
                hi = a.astype(BF16)
                lo = (a - hi.astype(F32)).astype(BF16)
                dn = (((1,), (1,)), ((), ()))
                v = lax.dot_general(ones, hi, dn, preferred_element_type=F32) + lax.dot_general(ones, lo, dn, preferred_element_type=F32)
                out.append(v[:1])
        out = jnp.concatenate(out + [zero4], 0)
        if box == 1:
            fown_ref[...] = out + jnp.concatenate([right[f, 4 * NP:4 * NP + 4, :] for f in range(3)] + [zero4], 0)
        else:
            fout_ref[NP if box == 0 else NP + 1] = out

def pair_forces(pos, par, own, ownpar, joined):
    v = pl.BlockSpec(memory_space=pltpu.VMEM)
    return pl.pallas_call(
        functools.partial(pair_kernel, joined),
        out_shape=(jax.ShapeDtypeStruct((NBR, 16, 128), F32), jax.ShapeDtypeStruct((16, 128), F32)),
        in_specs=[v] * 4, out_specs=(v, v),
        scratch_shapes=[
            pltpu.VMEM((6, 256, 8, 128), F32),
            pltpu.VMEM((6, -(-4 * RB // 8) * 8, 128), F32),
            pltpu.VMEM((3, 256, 8, 128), F32),
            pltpu.VMEM((56, 128), jnp.int32),
            pltpu.SMEM((56, 128), jnp.int32),
            pltpu.SemaphoreType.DMA,
        ],
        compiler_params=pltpu.CompilerParams(vmem_limit_bytes=32 << 20),
    )(pos, par, own, ownpar)


def hilbert(cells, bits):
    x = list(cells)
    q = 1 << (bits - 1)
    while q > 1:
        p = q - 1
        for i in range(3):
            hit = (x[i] & q) != 0
            if i == 0:
                x[0] = jnp.where(hit, x[0] ^ p, x[0])
            else:
                swap = (x[0] ^ x[i]) & p
                x[0], x[i] = jnp.where(hit, x[0] ^ p, x[0] ^ swap), jnp.where(hit, x[i], x[i] ^ swap)
        q >>= 1
    x[1] = x[1] ^ x[0]
    x[2] = x[2] ^ x[1]
    flip = jnp.zeros_like(x[0])
    q = 1 << (bits - 1)
    while q > 1:
        flip = jnp.where((x[2] & q) != 0, flip ^ (q - 1), flip)
        q >>= 1
    x = [v ^ flip for v in x]
    key = jnp.zeros_like(x[0])
    for bit in range(bits - 1, -1, -1):
        for a in range(3):
            key = key * 2 + ((x[a] >> bit) & 1)
    return key


def split3(a):
    hi = a.astype(BF16)
    rest = a - hi.astype(F32)
    mid = rest.astype(BF16)
    lo = (rest - mid.astype(F32)).astype(BF16)
    return jnp.concatenate([hi, mid, lo], 0)


def chosen(rank, t):
    place = lax.broadcasted_iota(jnp.int32, (TILE, TILE), 0) + TILE * t
    tiles = [(rank[j : j + 1, :] == place).astype(F32).astype(BF16) for j in range(4)]
    return jnp.concatenate(tiles, 1)


def sort_kernel(
    count_ref, eps_ref, sig_ref, pos_ref, vel_ref, frc_ref, chg_ref, typ_ref,
    x_ref, v_ref, rec_ref, rank_ref, stage, staged,
):
    v = vel_ref[...] + HALF_STEP * frc_ref[...]
    x = pos_ref[...] + TIME_STEP * v
    count = count_ref[0, 0]
    row = lax.broadcasted_iota(jnp.int32, (4, TILE), 0)
    live = row < count
    kinds = typ_ref[...]
    eps = jnp.zeros((4, TILE), F32)
    sig = jnp.zeros((4, TILE), F32)
    for k in range(eps_ref.shape[0]):
        eps = jnp.where(kinds == k, eps_ref[k], eps)
        sig = jnp.where(kinds == k, sig_ref[k], sig)
    alive = live.astype(F32)
    stage[...] = jnp.zeros_like(stage)
    stage[0:12, :] = x
    stage[12:24, :] = v
    stage[24:28, :] = chg_ref[...] * alive
    stage[28:32, :] = jnp.sqrt(eps) * alive
    stage[32:36, :] = sig
    cells = [
        jnp.clip((jnp.clip(x[4 * a : 4 * a + 4], -1.0, 2.0) * 4.0).astype(jnp.int32), 0, 3)
        for a in range(3)
    ]
    index = row * TILE + lax.broadcasted_iota(jnp.int32, (4, TILE), 1)
    key = jnp.where(live, hilbert(cells, 2), 64) * 512 + index
    key = jnp.concatenate([key.astype(F32), jnp.zeros((4, TILE), F32)], 0)
    down = jnp.transpose(key, (1, 0))
    ranks = []
    for j in range(4):
        less = jnp.zeros((TILE, TILE), F32)
        for i in range(4):
            less = less + (down[:, i : i + 1] < key[j : j + 1, :]).astype(F32)
        ranks.append(jnp.sum(less, axis=0, keepdims=True))
    rank = jnp.concatenate(ranks, 0).astype(jnp.int32)
    rank_ref[...] = rank
    fields = jnp.concatenate([stage[pl.ds(t, 16, stride=4), :] for t in range(4)], 1)
    parts = split3(fields)
    for t in range(4):
        out = lax.dot_general(
            parts, chosen(rank, t), (((1,), (1,)), ((), ())), preferred_element_type=F32
        )
        staged[pl.ds(t, 16, stride=4), :] = (out[32:48] + out[16:32]) + out[0:16]
    row16 = lax.broadcasted_iota(jnp.int32, (16, TILE), 0)
    place = staged[0:16, :]
    x_ref[...] = place
    v_ref[...] = staged[12:28, :]
    rec_ref[0] = jnp.where((row16 & 3) < count, place, FAR)
    rec_ref[1] = staged[24:40, :]


def there(offset, sign):
    return tuple(
        lax.rem(lax.axis_index(a) + sign * o + lax.axis_size(a), lax.axis_size(a))
        for a, o in zip(AXES, offset)
    )


def greet(devices):
    barrier = pltpu.get_barrier_semaphore()
    for device in devices:
        pl.semaphore_signal(barrier, inc=1, device_id=device, device_id_type=MESH)
    pl.semaphore_wait(barrier, len(devices))


def send(source, target, send_sem, recv_sem, device):
    return pltpu.make_async_remote_copy(
        src_ref=source,
        dst_ref=target,
        send_sem=send_sem,
        recv_sem=recv_sem,
        device_id=device,
        device_id_type=MESH,
    )


def spread_kernel(rec_ref, nbr_ref, send_sem, recv_sem):
    greet([there(d, 1) for d in OFFSETS])
    copies = [
        send(rec_ref, nbr_ref.at[k], send_sem.at[k], recv_sem.at[k], there(d, -1))
        for k, d in enumerate(OFFSETS)
    ]
    for copy in copies:
        copy.start()
    for copy in copies:
        copy.wait()


def turn_kernel(
    fout_ref, fown_ref, x_ref, v_ref, old_ref,
    nbr_ref, new_ref, x2_ref, v2_ref,
    back, send_sem, recv_sem, send2_sem, recv2_sem,
):
    around = {tuple(s * o for o in d) for d in OFFSETS for s in (1, -1)}
    greet([there(d, 1) for d in sorted(around)])
    copies = [
        send(fout_ref.at[k], back.at[k], send_sem.at[k], recv_sem.at[k], there(d, 1))
        for k, d in enumerate(OFFSETS)
    ]
    for copy in copies:
        copy.start()
    for copy in copies:
        copy.wait_recv()
    total = fown_ref[...]
    for k in range(NBR):
        total = total + back[k]
    v = v_ref[...] + HALF_STEP * total
    v = v + HALF_STEP * total
    x = x_ref[...] + TIME_STEP * v
    new_ref[...] = jnp.where(old_ref[0] > 0.1 * FAR, FAR, x)
    again = [
        send(new_ref, nbr_ref.at[k], send2_sem.at[k], recv2_sem.at[k], there(d, -1))
        for k, d in enumerate(OFFSETS)
    ]
    for copy in again:
        copy.start()
    x2_ref[...] = x
    v2_ref[...] = v
    for copy in copies:
        copy.wait_send()
    for copy in again:
        copy.wait()


def last_kernel(
    fout_ref, fown_ref, x_ref, v_ref, rank_ref, xo_ref, vo_ref, fo_ref,
    back, stage, onehot, send_sem, recv_sem,
):
    greet([there(d, -1) for d in OFFSETS])
    copies = [
        send(fout_ref.at[k], back.at[k], send_sem.at[k], recv_sem.at[k], there(d, 1))
        for k, d in enumerate(OFFSETS)
    ]
    for copy in copies:
        copy.start()
    rank = rank_ref[...]
    for t in range(4):
        onehot[TILE * t : TILE * t + TILE, :] = chosen(rank, t)
    for copy in copies:
        copy.wait()
    total = fown_ref[...]
    for k in range(NBR):
        total = total + back[k]
    stage[0:16, :] = x_ref[...]
    stage[12:28, :] = v_ref[...] + HALF_STEP * total
    stage[24:40, :] = total
    stage[36:64, :] = jnp.zeros((28, TILE), F32)
    fields = jnp.concatenate([stage[pl.ds(t, 16, stride=4), :] for t in range(4)], 1)
    out = jnp.dot(split3(fields), onehot[...], preferred_element_type=F32)
    out = (out[32:48] + out[16:32]) + out[0:16]
    xo_ref[...] = out[0:3]
    vo_ref[...] = out[3:6]
    fo_ref[...] = out[6:9]


def call(kernel, outs, scratch, collective=None, ins=None, count=0):
    vmem = pl.BlockSpec(memory_space=pltpu.VMEM)
    params = {"vmem_limit_bytes": 24 << 20}
    if collective is not None:
        params.update(collective_id=collective, has_side_effects=True)
    return pl.pallas_call(
        kernel,
        out_shape=tuple(jax.ShapeDtypeStruct(shape, kind) for shape, kind in outs),
        in_specs=[pl.BlockSpec(memory_space=pltpu.SMEM)] * count + [vmem] * (ins - count),
        out_specs=tuple(vmem for _ in outs),
        scratch_shapes=scratch,
        compiler_params=pltpu.CompilerParams(**params),
    )


def on_device(
    positions, velocities, forces, charges, atom_types, tile_counts, pair_epsilon, pair_sigma
):
    dma = pltpu.SemaphoreType.DMA((NBR,))
    rows = ((16, TILE), F32)
    x, v, rec, rank = call(
        sort_kernel,
        (rows, rows, ((2, 16, TILE), F32), ((4, TILE), jnp.int32)),
        [pltpu.VMEM((64, TILE), F32), pltpu.VMEM((64, TILE), F32)],
        ins=8,
        count=3,
    )(
        tile_counts.reshape(1, 1), pair_epsilon, pair_sigma,
        positions.reshape(12, TILE), velocities.reshape(12, TILE), forces.reshape(12, TILE),
        charges.reshape(4, TILE), atom_types.reshape(4, TILE),
    )
    (first,) = call(
        spread_kernel, (((NBR, 2, 16, TILE), F32),), [dma, dma], collective=0, ins=1
    )(rec)
    fout, fown = pair_forces(first, first, rec, rec, True)
    second, own, x, v = call(
        turn_kernel,
        (((NBR, 16, TILE), F32), rows, rows, rows),
        [pltpu.VMEM((NBR, 16, TILE), F32), dma, dma, dma, dma],
        collective=1,
        ins=5,
    )(fout, fown, x, v, rec)
    fout, fown = pair_forces(second, first, own, rec, False)
    flat = ((3, 4 * TILE), F32)
    outs = call(
        last_kernel,
        (flat, flat, flat),
        [pltpu.VMEM((NBR, 16, TILE), F32), pltpu.VMEM((64, TILE), F32),
         pltpu.VMEM((512, 512), BF16), dma, dma],
        collective=2,
        ins=5,
    )(fout, fown, x, v, rank)
    return tuple(out.reshape(3, 1, 1, 1, 4 * TILE) for out in outs)


def solution(mesh):
    atoms = P(None, "gx", "gy", "gz", None)
    in_specs = (
        atoms, atoms, atoms,
        P("gx", "gy", "gz", None),
        P("gx", "gy", "gz", None),
        P("gx", "gy", "gz"),
        P(), P(),
    )
    return jax.shard_map(
        on_device, mesh=mesh, in_specs=in_specs, out_specs=(atoms,) * 3, check_vma=False
    )
```

time: 273 us -> 88.2 us (0.32)
  the two profiles are of different devices: /device:TPU:6 before, /device:TPU:2 now
where the time goes in v1:
time: 88.2 us; the launch traced here: 88 us
  Pallas kernels  82.6 us (94%)
  local copies, waits for them, and re-layouts  3.86 us (4%)
  between operations  1.4 us (2%)
    pallas_call x2, Pallas kernels, pair_forces(): pl.pallas_call(functools.partial(pair_kernel, joined), out_shape=(jax.Sha...  24.2 us
    pallas_call x1, Pallas kernels, on_device(): call(spread_kernel, (((NBR, 2, 16, TILE), F32),), [dma, dma], collective=...  23.9 us
    pallas_call x1, Pallas kernels, on_device(): call(turn_kernel, (((NBR, 16, TILE), F32), rows, rows, rows), [pltpu.VMEM...  19 us
    pallas_call x1, Pallas kernels, on_device(): call(last_kernel, (flat, flat, flat), [pltpu.VMEM((NBR, 16, TILE), F32),...  14.3 us
    unnamed x17, local copies, waits for them, and re-layouts  3.83 us

profile of v1, /device:TPU:2, one launch (start us, length us, event | category | flops | bytes accessed | tf_op | source)
XLA Modules:
  0.0 88.0 jit_solution(6339977319070009347)
XLA Ops:
  0.6 0.0 copy-start.4
  1.3 0.0 copy-done.4
  1.4 0.0 copy-start.5
  1.4 0.7 copy-done.5
  2.1 0.0 copy-start.6
  2.1 0.7 copy-done.6
  2.8 0.0 copy-start
  2.8 0.0 copy-start.1
  2.8 0.0 copy-start.2
  2.8 0.0 copy-start.3
  2.9 0.6 copy-done
  3.5 0.0 copy-done.1
  3.5 0.0 copy-done.2
  3.5 0.0 copy-done.3
  3.5 1.1 %shard_map.103 = (f32[16,128]{1,0:T(8,128)S(1)}, f32[16,128]{1,0:T(8,128)S(1)}, f32[2,16,128]{2,1,0:T(8,128)S(1)}, s32[4,128]{1,0:T(4,128)S(1)}) custom-call(s32[1,1]{1,0:T(1,128)} %bitcast.6.count_ref, f32[32]{0:T(128)S(1)} %copy-done.2, f32[32]{0:T(128)S(1)} %copy-done.3, f32[12,128]{1,0:T(8,128)S(1)} %reshape.34.pos_ref, f32[12,128]{1,0:T(8,128)S(1)} %reshape.35.vel_ref, ...), custom_call_target="tpu_custom_call" | custom-call | tf_op jit(solution)/shard_map/pallas_call | solution.py:403
  4.6 23.9 %shard_map.104.pos_ref.par_ref = f32[6,2,16,128]{3,2,1,0:T(8,128)S(1)} custom-call(f32[2,16,128]{2,1,0:T(8,128)S(1)} %get-tuple-element.18.rec_ref.own_ref.ownpar_ref.old_ref), custom_call_target="tpu_custom_call" | custom-call | tf_op jit(solution)/shard_map/pallas_call | solution.py:414
  28.6 12.0 %shard_map.105 = (f32[6,16,128]{2,1,0:T(8,128)S(1)}, f32[16,128]{1,0:T(8,128)S(1)}) custom-call(f32[6,2,16,128]{3,2,1,0:T(8,128)S(1)} %shard_map.104.pos_ref.par_ref, f32[6,2,16,128]{3,2,1,0:T(8,128)S(1)} %shard_map.104.pos_ref.par_ref, f32[2,16,128]{2,1,0:T(8,128)S(1)} %get-tuple-element.18.rec_ref.own_ref.ownpar_ref.old_ref, ...), custom_call_target="tpu_custom_call" | custom-call | tf_op jit(solution)/shard_map/pallas_call | solution.py:168
  40.6 19.0 %shard_map.106 = (f32[6,16,128]{2,1,0:T(8,128)S(1)}, f32[16,128]{1,0:T(8,128)S(1)}, f32[16,128]{1,0:T(8,128)S(1)}, f32[16,128]{1,0:T(8,128)S(1)}) custom-call(f32[6,16,128]{2,1,0:T(8,128)S(1)} %get-tuple-element.19.fout_ref, f32[16,128]{1,0:T(8,128)S(1)} %get-tuple-element.20.fown_ref, f32[16,128]{1,0:T(8,128)S(1)} %get-tuple-element.21.x_ref, ...), custom_call_target="tpu_custom_call" | custom-call | tf_op jit(solution)/shard_map/pallas_call | solution.py:418
  59.6 12.2 %shard_map.107 = (f32[6,16,128]{2,1,0:T(8,128)S(1)}, f32[16,128]{1,0:T(8,128)S(1)}) custom-call(f32[6,16,128]{2,1,0:T(8,128)S(1)} %get-tuple-element.23.pos_ref, f32[6,2,16,128]{3,2,1,0:T(8,128)S(1)} %shard_map.104.pos_ref.par_ref, f32[16,128]{1,0:T(8,128)S(1)} %get-tuple-element.24.own_ref, ...), custom_call_target="tpu_custom_call" | custom-call | tf_op jit(solution)/shard_map/pallas_call | solution.py:168
  71.8 14.3 %shard_map.108 = (f32[3,512]{1,0:T(4,128)S(1)}, f32[3,512]{1,0:T(4,128)S(1)}, f32[3,512]{1,0:T(4,128)S(1)}) custom-call(f32[6,16,128]{2,1,0:T(8,128)S(1)} %get-tuple-element.25.fout_ref, f32[16,128]{1,0:T(8,128)S(1)} %get-tuple-element.26.fown_ref, f32[16,128]{1,0:T(8,128)S(1)} %get-tuple-element.27.x_ref, f32[16,128]{1,0:T(8,128)S(1)} %get-tuple-element.28.v_ref, ...), custom_call_target="tpu_custom_call" | custom-call | tf_op jit(solution)/shard_map/pallas_call | solution.py:427
  86.2 0.6 copy.11
  86.8 0.6 copy.12
  87.4 0.6 copy.13
  (6 shorter events, 0.1 us)
Async XLA Ops:
  0.6 0.7 copy-start.4
  1.4 0.7 copy-start.5
  2.1 0.7 copy-start.6
  2.8 0.7 copy-start
  2.8 0.7 copy-start.1
  2.8 0.7 copy-start.2
  2.8 0.7 copy-start.3

commit v2 on v1

v2 whole, which is shorter than its diff:
```python
import functools

import jax
import jax.numpy as jnp
from jax import lax
from jax.experimental import pallas as pl
from jax.experimental.pallas import tpu as pltpu
from jax.sharding import PartitionSpec as P

TILE = 128
STEPS = 2
TIME_STEP = 0.05
HALF_STEP = 0.025
PLATE = ((1, 0), (1, 1), (0, 1), (-1, 1), (-1, 0), (-1, -1), (0, -1), (1, -1))
NP = len(PLATE)
OFFSETS = tuple((x, y, 0) for x, y in PLATE) + ((0, 0, -1), (0, 0, 1))
NBR = NP + 2
AXES = ("gx", "gy", "gz")
MESH = pl.DeviceIdType.MESH
F32 = jnp.float32
BF16 = jnp.bfloat16
FAR = 1e6
RIGHTS = 4 * (NP + 2)
RROWS = RIGHTS + 8
UNROLL = 4
PAD = 12
LOG2E = 1.4426950408889634
FORCE = 8.0 / (3.24 * 3.24)


def shares(first, pos_ref, par_ref, own_ref, ownpar_ref):
    row = lax.broadcasted_iota(jnp.int32, (64, TILE), 0)
    col = lax.broadcasted_iota(jnp.int32, (64, TILE), 1)
    lane = lax.broadcasted_iota(jnp.int32, (1, TILE), 1) >> 2
    lt, lbox, rt, rbox = row >> 4, (row >> 2) & 3, col & 3, col >> 2
    own_n = ownpar_ref[1, 12:13, :]
    nr = own_n
    for j in range(NP):
        nr = jnp.where(lane == j, par_ref[j, 1, 12:13, :], nr)
    below_n, above_n = par_ref[NP, 1, 12:13, :], par_ref[NP + 1, 1, 12:13, :]
    nl = jnp.where(lbox == 0, below_n, jnp.where(lbox == 2, above_n, own_n))
    nr = jnp.broadcast_to(nr, (64, TILE))
    ahead = (rbox < NP // 2) | ((rbox == NP) & (lbox == 2))
    left_first = (rbox < NP // 2) | ((rbox == NP) & (lbox == 0))
    lf, rf = lt.astype(F32), rt.astype(F32)
    order = jnp.where(left_first, lf * nr + rf, rf * nl + lf)
    if first:
        w1 = jnp.where(left_first, nl, nr)
        w2 = jnp.where(left_first, nr, nl)
    else:
        mine = own_ref[14:15, :]
        below, same, above = mine, mine, mine
        for j in range(NP):
            hit = lane == j
            below = jnp.where(hit, pos_ref[j, 12:13, :], below)
            same = jnp.where(hit, pos_ref[j, 14:15, :], same)
            above = jnp.where(hit, pos_ref[j, 13:14, :], above)
        below = jnp.where(lane == NP, pos_ref[NP, 14:15, :], below)
        above = jnp.where(lane == NP, pos_ref[NP + 1, 14:15, :], above)
        other = jnp.where(lbox == 0, below, jnp.where(lbox == 2, above, same))
        mine = jnp.broadcast_to(mine, (64, TILE))
        w1 = jnp.where(ahead, mine, other)
        w2 = jnp.where(ahead, other, mine)
    w1, w2 = w1 * w1 * w1, w2 * w2 * w2
    inside = (order + 0.5) * (w1 + w2) < w2 * (nl * nr)
    takes = jnp.where(inside, 1.0, 0.0)
    takes = jnp.where(ahead, takes, 1.0 - takes)
    shared = ((rbox < NP) & (lbox < 3)) | ((rbox == NP) & ((lbox == 0) | (lbox == 2)))
    alone = ((rbox == NP) & (lbox == 1) & (lt < rt)) | ((rbox == NP + 1) & (lbox == 1) & (lt == rt))
    return jnp.where(shared, takes, jnp.where(alone, 1.0, 0.0))


def pair_kernel(
    joined, pos_ref, par_ref, own_ref, ownpar_ref, fout_ref, fown_ref,
    left, right, acc_left, acc_right, list_v, list_s, sem,
):
    position = (lambda k: pos_ref[k, 0]) if joined else (lambda k: pos_ref[k])
    own = own_ref[0] if joined else own_ref[...]
    row16 = lax.broadcasted_iota(jnp.int32, (16, 1), 0)
    lane16 = lax.broadcasted_iota(jnp.int32, (1, 16), 1)
    for k in range(NP + 2):
        if k < NP:
            p = position(k) + jnp.where(
                row16 < 4, float(PLATE[k][0]), jnp.where(row16 < 8, float(PLATE[k][1]), 0.0)
            )
            a = par_ref[k, 1]
        else:
            p, a = own, ownpar_ref[1]
        p = p * 2.0
        for f in range(3):
            right[f, 4 * k : 4 * k + 4, :] = p[4 * f : 4 * f + 4]
            right[3 + f, 4 * k : 4 * k + 4, :] = a[4 * f : 4 * f + 4]
    for f in range(6):
        right[f, RIGHTS:RROWS, :] = jnp.full((8, TILE), FAR if f < 3 else 0.0, F32)
    mins, maxs = [], []
    scale = jnp.where(lane16 < 4, 0.04 / 6.0 * FORCE, jnp.where(lane16 < 8, 4.0 * FORCE, 1.0))
    for box in range(3):
        if box == 1:
            p, a = own, ownpar_ref[1]
        else:
            slot = NP if box == 0 else NP + 1
            p = position(slot) + jnp.where(
                (row16 >= 8) & (row16 < 12), -1.0 if box == 0 else 1.0, 0.0
            )
            a = par_ref[slot, 1]
        down = jnp.transpose(jnp.concatenate([p * 2.0, a], 0), (1, 0))
        blocks = down[:, :16].reshape(4, 32, 16)
        mins.append(jnp.min(blocks, axis=1))
        maxs.append(jnp.max(blocks, axis=1))
        scaled = down[:, 16:] * scale
        for t in range(4):
            base = (t * 16 + box * 4) * 4
            for f in range(6):
                at = 4 * (f % 3) + t
                source = down if f < 3 else scaled
                left[f, base : base + 16] = jnp.broadcast_to(
                    source[:, at : at + 1], (TILE, TILE)
                ).reshape(16, 8, TILE)
    for f in range(6):
        left[f, 4 * PAD : 4 * PAD + 4] = jnp.full((4, 8, TILE), FAR if f < 3 else 0.0, F32)
    acc_left[...] = jnp.zeros_like(acc_left)
    acc_right[...] = jnp.zeros_like(acc_right)
    far = jnp.full((4, 16), FAR, F32)
    low = jnp.concatenate(mins + [far], 0)
    high = jnp.concatenate(maxs + [far], 0)
    gaps = jnp.zeros((64, TILE), F32)
    alive = None
    for f in range(3):
        a0 = jnp.concatenate([low[:, 4 * f + t : 4 * f + t + 1] for t in range(4)], 0)
        a1 = jnp.concatenate([high[:, 4 * f + t : 4 * f + t + 1] for t in range(4)], 0)
        v = jnp.concatenate([right[f], jnp.full((TILE - RROWS, TILE), FAR, F32)], 0)
        b0 = jnp.broadcast_to(jnp.min(v, axis=1, keepdims=True), (TILE, TILE))
        b1 = jnp.broadcast_to(jnp.max(v, axis=1, keepdims=True), (TILE, TILE))
        b0 = jnp.transpose(b0, (1, 0))[:1]
        b1 = jnp.transpose(b1, (1, 0))[:1]
        gap = jnp.maximum(jnp.maximum(a0 - b1, b0 - a1), 0.0)
        gaps = gaps + gap * gap
        if f == 0:
            alive = a0 < 0.1 * FAR
    near = (gaps < 3.2401) & alive & (shares(joined, pos_ref, par_ref, own_ref, ownpar_ref) > 0.5)
    row = lax.broadcasted_iota(jnp.int32, (64, TILE), 0)
    r64 = lax.broadcasted_iota(jnp.int32, (64, 64), 0)
    c64 = lax.broadcasted_iota(jnp.int32, (64, 64), 1)
    ones = near.astype(F32)
    before = jnp.dot(
        (c64 < r64).astype(F32).astype(BF16), ones.astype(BF16), preferred_element_type=F32
    )
    place = jnp.where(near, before.astype(jnp.int32), -1)
    lane = lax.broadcasted_iota(jnp.int32, (1, TILE), 1)
    count = jnp.maximum(jnp.sum(ones, axis=0, keepdims=True), 1.0)
    total = jnp.sum(jnp.where(lane < RIGHTS, count, 0.0), axis=1, keepdims=True)
    count = jnp.where(lane < RIGHTS, count, 1e6).astype(jnp.int32)
    value = row - PAD
    for w in range(12):
        word = jnp.zeros((1, TILE), jnp.int32)
        for j in range(4):
            hit = jnp.where(place == 4 * w + j, value, 0)
            word = word + (jnp.sum(hit, axis=0, keepdims=True) + PAD) * (64**j)
        list_v[w : w + 1, :] = word
    list_v[12:13, :] = count
    list_v[13:14, :] = jnp.broadcast_to(total, (1, TILE)).astype(jnp.int32)
    copy = pltpu.make_async_copy(list_v, list_s, sem)
    copy.start()
    copy.wait()

    def turn(_, state):
        r, k = state
        for _ in range(UNROLL):
            b = ((list_s[k >> 2, r] >> ((k & 3) * 6)) & 63) * 4
            at = pl.ds(b, 4)
            rx, ry, rz, rq, re, rs_ = [
                jnp.broadcast_to(right[f, pl.ds(r, 1), :], (8, TILE))[None] for f in range(6)
            ]
            dx = left[0, at] - rx
            dy = left[1, at] - ry
            dz = left[2, at] - rz
            s2 = (dx * dx + 0.09) + dy * dy + dz * dz
            rs = lax.rsqrt(s2)
            inv = rs * rs
            screen = jnp.exp2(s2 * (-LOG2E) * rs)
            w = jnp.maximum(3.33 - s2, 0.0)
            slope = (w * inv) * 1.5
            one = slope + 1.0
            two = one + slope
            size = left[5, at] + rs_
            ratio = size * size * inv
            cubed = ratio * ratio * ratio
            lennard = (left[4, at] * re) * cubed * (cubed * two - one)
            coulomb = (left[3, at] * rq) * screen * (rs * (one + 5.0) + slope)
            g = (lennard + coulomb) * w
            fx, fy, fz = g * dx, g * dy, g * dz
            acc_left[0, at] += fx
            acc_left[1, at] += fy
            acc_left[2, at] += fz
            acc_right[0, r] -= jnp.sum(fx, axis=0)
            acc_right[1, r] -= jnp.sum(fy, axis=0)
            acc_right[2, r] -= jnp.sum(fz, axis=0)
            on = k + 1 >= list_s[12, r]
            k = jnp.where(on, 0, k + 1)
            r = jnp.where(on, r + 1, r)
        return r, k

    lax.fori_loop(0, (list_s[13, 0] + UNROLL - 1) // UNROLL, turn, (jnp.int32(0), jnp.int32(0)))
    plate = par_ref[0, 1, 12:13, :]
    for k in range(1, NP):
        plate = plate + par_ref[k, 1, 12:13, :]
    tower = ownpar_ref[1, 12:13, :] + par_ref[NP, 1, 12:13, :] + par_ref[NP + 1, 1, 12:13, :]
    tail = jnp.broadcast_to(plate * tower, (4, TILE))

    def gathered(k):
        rows = [jnp.sum(acc_right[f, 4 * k : 4 * k + 4], axis=1) for f in range(3)]
        return jnp.concatenate(rows + [tail], 0)

    for k in range(NP):
        fout_ref[k] = gathered(k)
    unit = jnp.ones((8, TILE), BF16)
    for box in range(3):
        rows = []
        for f in range(3):
            for t in range(4):
                base = (t * 16 + box * 4) * 4
                a = acc_left[f, base : base + 16].reshape(TILE, TILE)
                hi = a.astype(BF16)
                lo = (a - hi.astype(F32)).astype(BF16)
                dims = (((1,), (1,)), ((), ()))
                v = lax.dot_general(unit, hi, dims, preferred_element_type=F32)
                v = v + lax.dot_general(unit, lo, dims, preferred_element_type=F32)
                rows.append(v[:1])
        out = jnp.concatenate(rows + [tail], 0)
        if box == 1:
            fown_ref[0:12, :] = (out + gathered(NP))[0:12]
            fown_ref[12:16, :] = tail
        else:
            fout_ref[NP if box == 0 else NP + 1] = out


def pair_forces(pos, par, own, ownpar, joined):
    vmem = pl.BlockSpec(memory_space=pltpu.VMEM)
    return pl.pallas_call(
        functools.partial(pair_kernel, joined),
        out_shape=(
            jax.ShapeDtypeStruct((NBR, 16, TILE), F32),
            jax.ShapeDtypeStruct((16, TILE), F32),
        ),
        in_specs=[vmem] * 4,
        out_specs=(vmem, vmem),
        scratch_shapes=[
            pltpu.VMEM((6, 256, 8, TILE), F32),
            pltpu.VMEM((6, RROWS, TILE), F32),
            pltpu.VMEM((3, 256, 8, TILE), F32),
            pltpu.VMEM((3, RROWS, 8, TILE), F32),
            pltpu.VMEM((16, TILE), jnp.int32),
            pltpu.SMEM((16, TILE), jnp.int32),
            pltpu.SemaphoreType.DMA,
        ],
        compiler_params=pltpu.CompilerParams(vmem_limit_bytes=24 << 20),
    )(pos, par, own, ownpar)


def hilbert(cells, bits):
    x = list(cells)
    q = 1 << (bits - 1)
    while q > 1:
        p = q - 1
        for i in range(3):
            hit = (x[i] & q) != 0
            if i == 0:
                x[0] = jnp.where(hit, x[0] ^ p, x[0])
            else:
                swap = (x[0] ^ x[i]) & p
                x[0], x[i] = jnp.where(hit, x[0] ^ p, x[0] ^ swap), jnp.where(hit, x[i], x[i] ^ swap)
        q >>= 1
    x[1] = x[1] ^ x[0]
    x[2] = x[2] ^ x[1]
    flip = jnp.zeros_like(x[0])
    q = 1 << (bits - 1)
    while q > 1:
        flip = jnp.where((x[2] & q) != 0, flip ^ (q - 1), flip)
        q >>= 1
    x = [v ^ flip for v in x]
    key = jnp.zeros_like(x[0])
    for bit in range(bits - 1, -1, -1):
        for a in range(3):
            key = key * 2 + ((x[a] >> bit) & 1)
    return key


def split3(a):
    hi = a.astype(BF16)
    rest = a - hi.astype(F32)
    mid = rest.astype(BF16)
    lo = (rest - mid.astype(F32)).astype(BF16)
    return jnp.concatenate([hi, mid, lo], 0)


def chosen(rank, t):
    place = lax.broadcasted_iota(jnp.int32, (TILE, TILE), 0) + TILE * t
    tiles = [(rank[j : j + 1, :] == place).astype(F32).astype(BF16) for j in range(4)]
    return jnp.concatenate(tiles, 1)


def sort_kernel(*refs):
    given, (x_ref, v_ref, rec_ref, rank_ref), held = refs[:8], refs[8:12], refs[12:20]
    stage, staged, sem = refs[20:]
    copies = [
        pltpu.make_async_copy(source, target, sem.at[i])
        for i, (source, target) in enumerate(zip(given, held))
    ]
    for copy in copies:
        copy.start()
    for copy in copies:
        copy.wait()
    pos_ref, vel_ref, frc_ref, chg_ref, typ_ref, count_ref, eps_ref, sig_ref = held

    def rows(ref, f):
        return [ref[f, 0, 0, :, TILE * t : TILE * t + TILE] for t in range(4)]

    def rows1(ref):
        return [ref[0, 0, :, TILE * t : TILE * t + TILE] for t in range(4)]

    def flat(ref):
        return jnp.concatenate([row for f in range(3) for row in rows(ref, f)], 0)

    v = flat(vel_ref) + HALF_STEP * flat(frc_ref)
    x = flat(pos_ref) + TIME_STEP * v
    count = count_ref[0, 0, 0]
    row = lax.broadcasted_iota(jnp.int32, (4, TILE), 0)
    live = row < count
    kinds = jnp.concatenate(rows1(typ_ref), 0)
    eps = jnp.zeros((4, TILE), F32)
    sig = jnp.zeros((4, TILE), F32)
    for k in range(eps_ref.shape[0]):
        eps = jnp.where(kinds == k, eps_ref[k], eps)
        sig = jnp.where(kinds == k, sig_ref[k], sig)
    alive = live.astype(F32)
    stage[...] = jnp.zeros_like(stage)
    stage[0:12, :] = x
    stage[12:24, :] = v
    stage[24:28, :] = jnp.concatenate(rows1(chg_ref), 0) * alive
    stage[28:32, :] = jnp.sqrt(eps) * alive
    stage[32:36, :] = sig
    cells = [
        jnp.clip((jnp.clip(x[4 * a : 4 * a + 4], -1.0, 2.0) * 4.0).astype(jnp.int32), 0, 3)
        for a in range(3)
    ]
    index = row * TILE + lax.broadcasted_iota(jnp.int32, (4, TILE), 1)
    key = jnp.where(live, hilbert(cells, 2), 64) * 512 + index
    key = jnp.concatenate([key.astype(F32), jnp.zeros((4, TILE), F32)], 0)
    down = jnp.transpose(key, (1, 0))
    ranks = []
    for j in range(4):
        less = jnp.zeros((TILE, TILE), F32)
        for i in range(4):
            less = less + (down[:, i : i + 1] < key[j : j + 1, :]).astype(F32)
        ranks.append(jnp.sum(less, axis=0, keepdims=True))
    rank = jnp.concatenate(ranks, 0).astype(jnp.int32)
    rank_ref[...] = rank
    fields = jnp.concatenate([stage[pl.ds(t, 16, stride=4), :] for t in range(4)], 1)
    parts = split3(fields)
    for t in range(4):
        out = lax.dot_general(
            parts, chosen(rank, t), (((1,), (1,)), ((), ())), preferred_element_type=F32
        )
        staged[pl.ds(t, 16, stride=4), :] = (out[32:48] + out[16:32]) + out[0:16]
    row16 = lax.broadcasted_iota(jnp.int32, (16, TILE), 0)
    place = staged[0:16, :]
    x_ref[...] = place
    v_ref[...] = staged[12:28, :]
    rec_ref[0] = jnp.where((row16 & 3) < count, place, FAR)
    rec_ref[1] = jnp.where(row16 < 12, staged[24:40, :], count.astype(F32))


def there(offset, sign):
    return tuple(
        lax.rem(lax.axis_index(a) + sign * o + lax.axis_size(a), lax.axis_size(a))
        for a, o in zip(AXES, offset)
    )


def greet(devices):
    barrier = pltpu.get_barrier_semaphore()
    for device in devices:
        pl.semaphore_signal(barrier, inc=1, device_id=device, device_id_type=MESH)
    pl.semaphore_wait(barrier, len(devices))


def send(source, target, send_sem, recv_sem, device):
    return pltpu.make_async_remote_copy(
        src_ref=source,
        dst_ref=target,
        send_sem=send_sem,
        recv_sem=recv_sem,
        device_id=device,
        device_id_type=MESH,
    )


def spread_kernel(rec_ref, nbr_ref, send_sem, recv_sem):
    greet([there(d, 1) for d in OFFSETS])
    copies = [
        send(rec_ref, nbr_ref.at[k], send_sem.at[k], recv_sem.at[k], there(d, -1))
        for k, d in enumerate(OFFSETS)
    ]
    for copy in copies:
        copy.start()
    for copy in copies:
        copy.wait()


def turn_kernel(
    fout_ref, fown_ref, x_ref, v_ref, old_ref,
    nbr_ref, new_ref, x2_ref, v2_ref,
    back, send_sem, recv_sem, send2_sem, recv2_sem,
):
    greet([there(d, 1) for d in OFFSETS])
    copies = [
        send(fout_ref.at[k], back.at[k], send_sem.at[k], recv_sem.at[k], there(d, 1))
        for k, d in enumerate(OFFSETS)
    ]
    for copy in copies:
        copy.start()
    for copy in copies:
        copy.wait_recv()
    total = fown_ref[...]
    for k in range(NBR):
        total = total + back[k]
    v = v_ref[...] + HALF_STEP * total
    v = v + HALF_STEP * total
    x = x_ref[...] + TIME_STEP * v
    row16 = lax.broadcasted_iota(jnp.int32, (16, TILE), 0)
    new = jnp.where(old_ref[0] > 0.1 * FAR, FAR, x)
    new = jnp.where(row16 == 12, back[NP + 1, 12:13, :], new)
    new = jnp.where(row16 == 13, back[NP, 12:13, :], new)
    new_ref[...] = jnp.where(row16 == 14, fown_ref[12:13, :], new)
    again = [
        send(new_ref, nbr_ref.at[k], send2_sem.at[k], recv2_sem.at[k], there(d, -1))
        for k, d in enumerate(OFFSETS)
    ]
    for copy in again:
        copy.start()
    x2_ref[...] = x
    v2_ref[...] = v
    for copy in copies:
        copy.wait_send()
    for copy in again:
        copy.wait()


def last_kernel(
    fout_ref, fown_ref, x_ref, v_ref, rank_ref, xo_ref, vo_ref, fo_ref,
    back, stage, onehot, send_sem, recv_sem,
):
    greet([there(d, -1) for d in OFFSETS])
    copies = [
        send(fout_ref.at[k], back.at[k], send_sem.at[k], recv_sem.at[k], there(d, 1))
        for k, d in enumerate(OFFSETS)
    ]
    for copy in copies:
        copy.start()
    rank = rank_ref[...]
    for t in range(4):
        onehot[TILE * t : TILE * t + TILE, :] = chosen(rank, t)
    for copy in copies:
        copy.wait()
    total = fown_ref[...]
    for k in range(NBR):
        total = total + back[k]
    stage[0:16, :] = x_ref[...]
    stage[12:28, :] = v_ref[...] + HALF_STEP * total
    stage[24:40, :] = total
    stage[36:64, :] = jnp.zeros((28, TILE), F32)
    fields = jnp.concatenate([stage[pl.ds(t, 16, stride=4), :] for t in range(4)], 1)
    out = jnp.dot(split3(fields), onehot[...], preferred_element_type=F32)
    out = (out[32:48] + out[16:32]) + out[0:16]
    for f in range(3):
        xo_ref[f, 0, 0] = out[f : f + 1]
        vo_ref[f, 0, 0] = out[3 + f : 4 + f]
        fo_ref[f, 0, 0] = out[6 + f : 7 + f]


def place_kernel(*refs):
    copies = [pltpu.make_async_copy(refs[i], refs[3 + i], refs[6].at[i]) for i in range(3)]
    for copy in copies:
        copy.start()
    for copy in copies:
        copy.wait()


def call(kernel, outs, scratch, collective=None, ins=None, raw_in=False, raw_out=False, limit=24 << 20):
    vmem = pl.BlockSpec(memory_space=pltpu.VMEM)
    hbm = pl.BlockSpec(memory_space=pltpu.HBM)
    params = {"vmem_limit_bytes": limit}
    if collective is not None:
        params.update(collective_id=collective, has_side_effects=True)
    return pl.pallas_call(
        kernel,
        out_shape=tuple(jax.ShapeDtypeStruct(shape, kind) for shape, kind in outs),
        in_specs=[hbm if raw_in else vmem] * ins,
        out_specs=tuple(hbm if raw_out else vmem for _ in outs),
        scratch_shapes=scratch,
        compiler_params=pltpu.CompilerParams(**params),
    )


def on_device(
    positions, velocities, forces, charges, atom_types, tile_counts, pair_epsilon, pair_sigma
):
    dma = pltpu.SemaphoreType.DMA((NBR,))
    rows = ((16, TILE), F32)
    wide = (positions, velocities, forces, charges, atom_types)
    small = (tile_counts, pair_epsilon, pair_sigma)
    x, v, rec, rank = call(
        sort_kernel,
        (rows, rows, ((2, 16, TILE), F32), ((4, TILE), jnp.int32)),
        [pltpu.VMEM(given.shape, given.dtype) for given in wide]
        + [pltpu.SMEM(given.shape, given.dtype) for given in small]
        + [pltpu.VMEM((64, TILE), F32), pltpu.VMEM((64, TILE), F32), pltpu.SemaphoreType.DMA((8,))],
        ins=8,
        raw_in=True,
        limit=67043328,
    )(
        *wide, *small
    )
    (first,) = call(
        spread_kernel, (((NBR, 2, 16, TILE), F32),), [dma, dma], collective=0, ins=1
    )(rec)
    fout, fown = pair_forces(first, first, rec, rec, True)
    second, own, x, v = call(
        turn_kernel,
        (((NBR, 16, TILE), F32), rows, rows, rows),
        [pltpu.VMEM((NBR, 16, TILE), F32), dma, dma, dma, dma],
        collective=1,
        ins=5,
    )(fout, fown, x, v, rec)
    fout, fown = pair_forces(second, first, own, rec, False)
    flat = ((3, 1, 1, 1, 4 * TILE), F32)
    outs = call(
        last_kernel,
        (flat, flat, flat),
        [pltpu.VMEM((NBR, 16, TILE), F32), pltpu.VMEM((64, TILE), F32),
         pltpu.VMEM((512, 512), BF16), dma, dma],
        collective=2,
        ins=5,
    )(fout, fown, x, v, rank)
    return call(
        place_kernel, (flat, flat, flat), [pltpu.SemaphoreType.DMA((3,))], ins=3, raw_out=True
    )(*outs)


def solution(mesh):
    atoms = P(None, "gx", "gy", "gz", None)
    in_specs = (
        atoms, atoms, atoms,
        P("gx", "gy", "gz", None),
        P("gx", "gy", "gz", None),
        P("gx", "gy", "gz"),
        P(), P(),
    )
    return jax.shard_map(
        on_device, mesh=mesh, in_specs=in_specs, out_specs=(atoms,) * 3, check_vma=False
    )
```

time: 88.2 us -> 87 us (0.986)
  the two profiles are of different devices: /device:TPU:2 before, /device:TPU:6 now
where the time goes in v2:
time: 87 us; the launch traced here: 85.7 us
  Pallas kernels  82.9 us (95%)
  local copies, waits for them, and re-layouts  1.4 us (2%)
  between operations  1.39 us (2%)
    pallas_call x2, Pallas kernels, pair_forces(): pl.pallas_call(functools.partial(pair_kernel, joined), out_shape=(jax.Sha...  28.3 us
    pallas_call x1, Pallas kernels, on_device(): call(spread_kernel, (((NBR, 2, 16, TILE), F32),), [dma, dma], collective=...  25.2 us
    pallas_call x1, Pallas kernels, on_device(): call(turn_kernel, (((NBR, 16, TILE), F32), rows, rows, rows), [pltpu.VMEM...  16.2 us
    pallas_call x1, Pallas kernels, on_device(): call(last_kernel, (flat, flat, flat), [pltpu.VMEM((NBR, 16, TILE), F32),...  10.4 us
    pallas_call x1, Pallas kernels, on_device(): call(sort_kernel, (rows, rows, ((2, 16, TILE), F32), ((4, TILE), jnp.int3...  2.14 us

profile of v2, /device:TPU:6, one launch (start us, length us, event | category | flops | bytes accessed | tf_op | source)
XLA Modules:
  0.0 85.7 jit_solution(8901240029150552788)
XLA Ops:
  1.3 2.1 %shard_map.103 = (f32[16,128]{1,0:T(8,128)}, f32[16,128]{1,0:T(8,128)}, f32[2,16,128]{2,1,0:T(8,128)}, s32[4,128]{1,0:T(4,128)}) custom-call(f32[3,1,1,1,512]{4,3,2,1,0:T(1,128)} %refs_0_.1, f32[3,1,1,1,512]{4,3,2,1,0:T(1,128)} %refs_1_.1, f32[3,1,1,1,512]{4,3,2,1,0:T(1,128)} %refs_2_.1, f32[1,1,1,512]{3,2,1,0:T(1,128)} %refs_3_.1, ...), custom_call_target="tpu_custom_call" | custom-call | tf_op jit(solution)/shard_map/pallas_call | solution.py:512
  3.4 0.0 copy-start
  3.4 0.7 copy-done
  4.1 25.2 %shard_map.104.pos_ref.par_ref = f32[10,2,16,128]{3,2,1,0:T(8,128)S(1)} custom-call(f32[2,16,128]{2,1,0:T(8,128)S(1)} %copy-done), custom_call_target="tpu_custom_call" | custom-call | tf_op jit(solution)/shard_map/pallas_call | solution.py:524
  29.4 0.0 copy-start.1
  29.4 0.0 copy-start.2
  29.4 0.0 copy-start.3
  29.4 13.6 %shard_map.105 = (f32[10,16,128]{2,1,0:T(8,128)S(1)}, f32[16,128]{1,0:T(8,128)S(1)}) custom-call(f32[10,2,16,128]{3,2,1,0:T(8,128)S(1)} %shard_map.104.pos_ref.par_ref, f32[10,2,16,128]{3,2,1,0:T(8,128)S(1)} %shard_map.104.pos_ref.par_ref, f32[2,16,128]{2,1,0:T(8,128)S(1)} %copy-done, f32[2,16,128]{2,1,0:T(8,128)S(1)} %copy-done), custom_call_target="tpu_custom_call" | custom-call | tf_op jit(solution)/shard_map/pallas_call | solution.py:239
  43.0 0.0 copy-done.1
  43.0 0.0 copy-done.2
  43.0 0.0 copy-done.3
  43.1 16.2 %shard_map.106 = (f32[10,16,128]{2,1,0:T(8,128)S(1)}, f32[16,128]{1,0:T(8,128)S(1)}, f32[16,128]{1,0:T(8,128)S(1)}, f32[16,128]{1,0:T(8,128)S(1)}) custom-call(f32[10,16,128]{2,1,0:T(8,128)S(1)} %get-tuple-element.19.fout_ref, f32[16,128]{1,0:T(8,128)S(1)} %get-tuple-element.20.fown_ref, f32[16,128]{1,0:T(8,128)S(1)} %copy-done.2, f32[16,128]{1,0:T(8,128)S(1)} %copy-done.3, ...), custom_call_target="tpu_custom_call" | custom-call | tf_op jit(solution)/shard_map/pallas_call | solution.py:528
  59.2 14.7 %shard_map.107 = (f32[10,16,128]{2,1,0:T(8,128)S(1)}, f32[16,128]{1,0:T(8,128)S(1)}) custom-call(f32[10,16,128]{2,1,0:T(8,128)S(1)} %get-tuple-element.23.pos_ref, f32[10,2,16,128]{3,2,1,0:T(8,128)S(1)} %shard_map.104.pos_ref.par_ref, f32[16,128]{1,0:T(8,128)S(1)} %get-tuple-element.24.own_ref, f32[2,16,128]{2,1,0:T(8,128)S(1)} %copy-done.1), custom_call_target="tpu_custom_call" | custom-call | tf_op jit(solution)/shard_map/pallas_call | solution.py:239
  73.9 0.0 copy-start.4
  73.9 0.7 copy-done.4
  74.6 10.4 %shard_map.108 = (f32[3,1,1,1,512]{4,3,2,1,0:T(1,128)S(1)}, f32[3,1,1,1,512]{4,3,2,1,0:T(1,128)S(1)}, f32[3,1,1,1,512]{4,3,2,1,0:T(1,128)S(1)}) custom-call(f32[10,16,128]{2,1,0:T(8,128)S(1)} %get-tuple-element.25.fout_ref, f32[16,128]{1,0:T(8,128)S(1)} %get-tuple-element.26.fown_ref, f32[16,128]{1,0:T(8,128)S(1)} %get-tuple-element.27.x_ref, ...), custom_call_target="tpu_custom_call" | custom-call | tf_op jit(solution)/shard_map/pallas_call | solution.py:537
  85.0 0.6 shard_map.109
Async XLA Ops:
  3.4 0.7 copy-start
  29.4 13.7 %copy-start.1 = (f32[2,16,128]{2,1,0:T(8,128)S(1)}, f32[2,16,128]{2,1,0:T(8,128)}, u32[]{:S(2)}) copy-start(f32[2,16,128]{2,1,0:T(8,128)} %get-tuple-element.18.rec_ref.own_ref.ownpar_ref.old_ref) | copy-start | bytes 49156
  29.4 13.7 %copy-start.2 = (f32[16,128]{1,0:T(8,128)S(1)}, f32[16,128]{1,0:T(8,128)}, u32[]{:S(2)}) copy-start(f32[16,128]{1,0:T(8,128)} %get-tuple-element.21.x_ref) | copy-start | bytes 24580
  29.4 13.7 %copy-start.3 = (f32[16,128]{1,0:T(8,128)S(1)}, f32[16,128]{1,0:T(8,128)}, u32[]{:S(2)}) copy-start(f32[16,128]{1,0:T(8,128)} %get-tuple-element.22.v_ref) | copy-start | bytes 24580
  73.9 0.7 copy-start.4
